TPU v7x, 32 devices: a whole 2x2x4 slice. The times are simulated.
32 devices in a mesh: dp: 4 (over x, core), row: 4 (over z), col: 2 (over y).
Axes of the slice: x: 2, y: 2, z: 4, core: 2. Of those that a mesh axis runs over, the one named last changes fastest.
Arguments:
- tokens_in: bfloat16 [8192, 768], P(('dp', 'col'), 'row'), may hold values from -6 to 6
- out_cot: bfloat16 [8192, 768], P(('dp', 'col'), 'row'), may hold values from -6 to 6
- segments: int32 [16, 512], P('dp'), may hold values from 0 to 31, never falling along the last dimension, each value on 1 to 256 neighbouring positions
- norm_params: float32 [4, 768], P(None, 'row'), may hold values from -1.2 to 1.5, as said below
- qkv_weight: float32 [768, 2304], P('row', 'col'), may hold values from -0.21875 to 0.21875
- proj_weight: float32 [768, 768], P('col', 'row'), may hold values from -0.875 to 0.875
- up_weight: float32 [768, 3072], P('row', 'col'), may hold values from -0.21875 to 0.21875
- down_weight: float32 [3072, 768], P('col', 'row'), may hold values from -0.109375 to 0.109375
- norm_first: float32 [4, 768], P(None, 'row'), may hold values from -18 to 18
- norm_second: float32 [4, 768], P(None, 'row'), may hold values from 30 to 300
- qkv_first: float32 [768, 2304], P('row', 'col'), may hold values from -18 to 18
- qkv_second: float32 [768, 2304], P('row', 'col'), may hold values from 30 to 300
- proj_first: float32 [768, 768], P('col', 'row'), may hold values from -18 to 18
- proj_second: float32 [768, 768], P('col', 'row'), may hold values from 30 to 300
- up_first: float32 [768, 3072], P('row', 'col'), may hold values from -18 to 18
- up_second: float32 [768, 3072], P('row', 'col'), may hold values from 30 to 300
- down_first: float32 [3072, 768], P('col', 'row'), may hold values from -18 to 18
- down_second: float32 [3072, 768], P('col', 'row'), may hold values from 30 to 300
Outputs:
- output: bfloat16 [8192, 768], P(('dp', 'col'), 'row')
- input_grad: bfloat16 [8192, 768], P(('dp', 'col'), 'row')
- norm_grad: float32 [4, 768], P(None, 'row')
- qkv_grad: float32 [768, 2304], P('row', 'col')
- proj_grad: float32 [768, 768], P('col', 'row')
- up_grad: float32 [768, 3072], P('row', 'col')
- down_grad: float32 [3072, 768], P('col', 'row')
- norm_new: float32 [4, 768], P(None, 'row')
- qkv_new: float32 [768, 2304], P('row', 'col')
- proj_new: float32 [768, 768], P('col', 'row')
- up_new: float32 [768, 3072], P('row', 'col')
- down_new: float32 [3072, 768], P('col', 'row')
- norm_first_new: float32 [4, 768], P(None, 'row')
- norm_second_new: float32 [4, 768], P(None, 'row')
- qkv_first_new: float32 [768, 2304], P('row', 'col')
- qkv_second_new: float32 [768, 2304], P('row', 'col')
- proj_first_new: float32 [768, 768], P('col', 'row')
- proj_second_new: float32 [768, 768], P('col', 'row')
- up_first_new: float32 [768, 3072], P('row', 'col')
- up_second_new: float32 [768, 3072], P('row', 'col')
- down_first_new: float32 [3072, 768], P('col', 'row')
- down_second_new: float32 [3072, 768], P('col', 'row')
Inputs may be any that keep to these rules, and one draw needn't show every extreme that they name: `segments`: within a row the numbers never fall; no number covers more than 256 positions of a row, and one covers exactly that many. `norm_params`: rows 0 and 2 lie in 0.5 to 1.5.
All inputs are finite; a program needn't handle non-finite values.
Results may differ from a plain program's by a relative error of at most 0.0093.
Values may be sent and summed in bfloat16 or wider, within the bound.
A program may use at most 192 MiB of HBM per device.

v0:
```python
import math

import jax
import jax.numpy as jnp
from jax import lax
from jax.sharding import PartitionSpec as P

D = 768
HEAD_DIM = 64
ROT_DIM = 16
SEQ_LEN = 512
STEP = 3


norm_eps = 1e-05
rotary_base = 10000.0
learn_rate = 0.01
beta_first = 0.9
beta_second = 0.95
adam_eps = 1e-08
decay_rate = 0.1
mask_fill = -1e30
inv_sqrt_two = 0.7071067811865476
inv_sqrt_two_pi = 0.3989422804014327


def gelu_value(value):
    return 0.5 * value * (1.0 + lax.erf(value * inv_sqrt_two))


def gelu_slope(value):
    return 0.5 * (1.0 + lax.erf(value * inv_sqrt_two)) + value * inv_sqrt_two_pi * jnp.exp(
        -0.5 * value * value
    )


def positions_of(segs):
    length = segs.shape[-1]
    index = jnp.broadcast_to(jnp.arange(length, dtype=jnp.int32), segs.shape)
    starts = jnp.concatenate(
        [jnp.ones(segs.shape[:-1] + (1,), bool), segs[..., 1:] != segs[..., :-1]], -1
    )
    first = lax.cummax(jnp.where(starts, index, 0), axis=segs.ndim - 1)
    return index - first


def rotary_tables(positions):
    half = ROT_DIM // 2
    freq = rotary_base ** (-2.0 * jnp.arange(half, dtype=jnp.float32) / ROT_DIM)
    angle = positions.astype(jnp.float32)[..., None] * freq
    return (jnp.cos(angle), jnp.sin(angle))


def rotate(tensor, cosine, sine):
    half = ROT_DIM // 2
    cos_part = cosine[..., None, :]
    sin_part = sine[..., None, :]
    front = tensor[..., :half]
    back = tensor[..., half:ROT_DIM]
    return jnp.concatenate(
        [
            front * cos_part - back * sin_part,
            back * cos_part + front * sin_part,
            tensor[..., ROT_DIM:],
        ],
        -1,
    )


def rotate_back(grad, cosine, sine):
    half = ROT_DIM // 2
    cos_part = cosine[..., None, :]
    sin_part = sine[..., None, :]
    front = grad[..., :half]
    back = grad[..., half:ROT_DIM]
    return jnp.concatenate(
        [
            front * cos_part + back * sin_part,
            back * cos_part - front * sin_part,
            grad[..., ROT_DIM:],
        ],
        -1,
    )


def masked_scores(query, keys, segment):
    length = segment.shape[0]
    scores = jnp.einsum(
        "qhd,khd->hqk", query, keys, preferred_element_type=jnp.float32
    ) / math.sqrt(HEAD_DIM)
    index = jnp.arange(length, dtype=jnp.int32)
    allowed = (segment[:, None] == segment[None, :]) & (index[None, :] <= index[:, None])
    return jnp.where(allowed[None], scores, mask_fill)


def attend(query, keys, values, segment):
    scores = masked_scores(query, keys, segment)
    total = jnp.sum(jnp.exp(scores), -1, keepdims=True)
    logsum = jnp.log(total)
    weights = jnp.exp(scores - logsum).astype(jnp.bfloat16)
    mixed = jnp.einsum("hqk,khd->qhd", weights, values, preferred_element_type=jnp.float32).astype(
        jnp.bfloat16
    )
    return (mixed, logsum[..., 0])


def attend_back(query, keys, values, segment, logsum, mixed, grad_mixed):
    scores = masked_scores(query, keys, segment)
    probs = jnp.exp(scores - logsum[..., None])
    weights = probs.astype(jnp.bfloat16)
    value_grad = jnp.einsum("hqk,qhd->khd", weights, grad_mixed, preferred_element_type=jnp.float32)
    prod_grad = jnp.einsum("qhd,khd->hqk", grad_mixed, values, preferred_element_type=jnp.float32)
    delta = jnp.sum(grad_mixed.astype(jnp.float32) * mixed.astype(jnp.float32), -1).T
    score_grad = (probs * (prod_grad - delta[..., None]) / math.sqrt(HEAD_DIM)).astype(jnp.bfloat16)
    query_grad = jnp.einsum("hqk,khd->qhd", score_grad, keys, preferred_element_type=jnp.float32)
    key_grad = jnp.einsum("hqk,qhd->khd", score_grad, query, preferred_element_type=jnp.float32)
    return (query_grad, key_grad, value_grad)


def dot32(left, right):
    return jnp.dot(left, right, preferred_element_type=jnp.float32)


def dot_rows(left, right):
    return lax.dot_general(
        left, right, (((0,), (0,)), ((), ())), preferred_element_type=jnp.float32
    )


def dot_cols(left, right):
    return lax.dot_general(
        left, right, (((1,), (1,)), ((), ())), preferred_element_type=jnp.float32
    )


def adam_update(weight, first, second, grad, decay):
    first_new = beta_first * first + (1.0 - beta_first) * grad
    second_new = beta_second * second + (1.0 - beta_second) * grad * grad
    first_hat = first_new / (1.0 - beta_first**STEP)
    second_hat = second_new / (1.0 - beta_second**STEP)
    weight_new = weight - learn_rate * (
        first_hat / (jnp.sqrt(second_hat) + adam_eps) + decay * weight
    )
    return (weight_new, first_new, second_new)


def gather_weight(piece):
    rows = piece.shape[0] // lax.axis_size("dp")
    own = lax.dynamic_slice_in_dim(piece, lax.axis_index("dp") * rows, rows, 0)
    return lax.all_gather(own, ("row", "dp"), axis=0, tiled=True)


def reduce_weights(grads):
    whole = jnp.concatenate([grad.astype(jnp.bfloat16) for grad in grads], 1)
    part = lax.psum_scatter(whole, ("row", "dp"), scatter_dimension=0, tiled=True)
    sums, start = [], 0
    for grad in grads:
        piece = part[:, start : start + grad.shape[1]]
        sums.append(lax.all_gather(piece, "dp", axis=0, tiled=True).astype(jnp.float32))
        start += grad.shape[1]
    return sums


def on_device(
    tokens_in,
    out_cot,
    segments,
    norm_params,
    qkv_weight,
    proj_weight,
    up_weight,
    down_weight,
    norm_first,
    norm_second,
    qkv_first,
    qkv_second,
    proj_first,
    proj_second,
    up_first,
    up_second,
    down_first,
    down_second,
):
    row_count = lax.axis_size("row")
    row_index = lax.axis_index("row")
    col_count = lax.axis_size("col")
    col_index = lax.axis_index("col")
    local_count, local_width = tokens_in.shape
    heads_here = qkv_weight.shape[1] // (3 * HEAD_DIM)
    seq_count = segments.shape[0] // row_count
    group_count = local_count * col_count
    share = group_count // row_count
    width = local_width * row_count
    bf16 = jnp.bfloat16

    def to_tokens(rows):
        blocks = rows.reshape(row_count, share, local_width)
        blocks = lax.all_to_all(blocks, "row", 0, 0, tiled=True)
        return jnp.moveaxis(blocks, 0, 1).reshape(share, width)

    x16 = to_tokens(lax.all_gather(tokens_in, "col", axis=0, tiled=True))
    cot16 = to_tokens(lax.all_gather(out_cot, "col", axis=0, tiled=True))
    norm_full = lax.all_gather(norm_params, "row", axis=1, tiled=True)
    pieces = (qkv_weight, up_weight, proj_weight.T, down_weight.T)
    all16 = gather_weight(jnp.concatenate([piece.astype(bf16) for piece in pieces], 1))
    first_cut = qkv_weight.shape[1]
    second_cut = first_cut + up_weight.shape[1]
    qkv16 = all16[:, :first_cut]
    up16 = all16[:, first_cut:second_cut]
    out16 = all16[:, second_cut:]

    xfull = x16.astype(jnp.float32)
    mean = jnp.sum(xfull, 1, keepdims=True) / D
    spread = jnp.sum(xfull * xfull, 1, keepdims=True) / D - mean * mean
    rstd = lax.rsqrt(spread + norm_eps)
    normed = (xfull - mean) * rstd
    first_in = (normed * norm_full[0] + norm_full[1]).astype(bf16)
    second_in = (normed * norm_full[2] + norm_full[3]).astype(bf16)
    qkv_own = dot32(first_in, qkv16)
    hidden_here = dot32(second_in, up16)

    width_qkv = qkv16.shape[1]
    seg_own = lax.dynamic_slice_in_dim(segments, row_index * seq_count, seq_count, 0)
    cosine, sine = rotary_tables(positions_of(seg_own))
    packed = qkv_own.reshape(seq_count, SEQ_LEN, heads_here, 3, HEAD_DIM)
    query = rotate(packed[..., 0, :], cosine, sine).astype(bf16)
    keys = rotate(packed[..., 1, :], cosine, sine).astype(bf16)
    values = packed[..., 2, :].astype(bf16)
    attended, logsum = lax.map(lambda item: attend(*item), (query, keys, values, seg_own))
    attn_width = heads_here * HEAD_DIM
    attn_flat = attended.reshape(share, attn_width)
    active = gelu_value(hidden_here).astype(bf16)
    act_cat = jnp.concatenate([attn_flat, active], 1)
    out_part = dot_cols(act_cat, out16)
    out_grad = dot_rows(cot16, act_cat)
    act_grad = dot32(cot16, out16)
    attended_grad = act_grad[:, :attn_width].astype(bf16)
    hidden_grad = (act_grad[:, attn_width:] * gelu_slope(hidden_here)).astype(bf16)
    up_grad = dot_rows(second_in, hidden_grad)
    grad_heads = attended_grad.reshape(seq_count, SEQ_LEN, heads_here, HEAD_DIM)
    query_grad, key_grad, value_grad = lax.map(
        lambda item: attend_back(*item),
        (query, keys, values, seg_own, logsum, attended, grad_heads),
    )
    query_grad = rotate_back(query_grad, cosine, sine)
    key_grad = rotate_back(key_grad, cosine, sine)
    packed_grad = (
        jnp.stack([query_grad, key_grad, value_grad], 3).reshape(share, width_qkv).astype(bf16)
    )
    qkv_grad = dot_rows(first_in, packed_grad)
    qkv_grad, up_grad, out_grad = reduce_weights((qkv_grad, up_grad, out_grad))
    first_grad = dot_cols(packed_grad, qkv16)
    second_grad = dot_cols(hidden_grad, up16)
    norm_part = jnp.stack(
        [
            jnp.sum(first_grad * normed, 0),
            jnp.sum(first_grad, 0),
            jnp.sum(second_grad * normed, 0),
            jnp.sum(second_grad, 0),
        ],
        0,
    )
    combined = norm_full[0] * first_grad + norm_full[2] * second_grad
    back_first = jnp.sum(combined, 1, keepdims=True) / D
    back_second = jnp.sum(combined * normed, 1, keepdims=True) / D
    grad_part = rstd * (combined - back_first - normed * back_second)

    def to_features(part):
        blocks = part.astype(bf16).reshape(share, row_count, local_width)
        blocks = lax.all_to_all(jnp.moveaxis(blocks, 1, 0), "row", 0, 0, tiled=True)
        parts = blocks.reshape(col_count, local_count, local_width)
        total = lax.dynamic_index_in_dim(parts, col_index, 0, keepdims=False).astype(jnp.float32)
        for step in range(1, col_count):
            peer = lax.rem(col_index + step, col_count)
            sent = lax.dynamic_index_in_dim(parts, peer, 0, keepdims=False)
            ring = [(i, (i + step) % col_count) for i in range(col_count)]
            total = total + lax.ppermute(sent, "col", ring).astype(jnp.float32)
        return total

    output = (tokens_in.astype(jnp.float32) + to_features(out_part)).astype(bf16)
    input_grad = (out_cot.astype(jnp.float32) + to_features(grad_part)).astype(bf16)
    norm_grad = lax.dynamic_slice_in_dim(
        lax.psum(norm_part, ("dp", "row", "col")), row_index * local_width, local_width, 1
    )
    proj_grad = out_grad[:, :attn_width].T
    down_grad = out_grad[:, attn_width:].T
    norm_new, norm_first_new, norm_second_new = adam_update(
        norm_params, norm_first, norm_second, norm_grad, 0.0
    )
    qkv_new, qkv_first_new, qkv_second_new = adam_update(
        qkv_weight, qkv_first, qkv_second, qkv_grad, decay_rate
    )
    proj_new, proj_first_new, proj_second_new = adam_update(
        proj_weight, proj_first, proj_second, proj_grad, decay_rate
    )
    up_new, up_first_new, up_second_new = adam_update(
        up_weight, up_first, up_second, up_grad, decay_rate
    )
    down_new, down_first_new, down_second_new = adam_update(
        down_weight, down_first, down_second, down_grad, decay_rate
    )
    return (
        output,
        input_grad,
        norm_grad,
        qkv_grad,
        proj_grad,
        up_grad,
        down_grad,
        norm_new,
        qkv_new,
        proj_new,
        up_new,
        down_new,
        norm_first_new,
        norm_second_new,
        qkv_first_new,
        qkv_second_new,
        proj_first_new,
        proj_second_new,
        up_first_new,
        up_second_new,
        down_first_new,
        down_second_new,
    )


def solution(mesh):
    placed = (
        P(("dp", "col"), "row"),
        P(("dp", "col"), "row"),
        P("dp", None),
        P(None, "row"),
        P("row", "col"),
        P("col", "row"),
        P("row", "col"),
        P("col", "row"),
        P(None, "row"),
        P(None, "row"),
        P("row", "col"),
        P("row", "col"),
        P("col", "row"),
        P("col", "row"),
        P("row", "col"),
        P("row", "col"),
        P("col", "row"),
        P("col", "row"),
    )
    return jax.shard_map(
        on_device,
        mesh=mesh,
        in_specs=placed,
        out_specs=(
            P(("dp", "col"), "row"),
            P(("dp", "col"), "row"),
            P(None, "row"),
            P("row", "col"),
            P("col", "row"),
            P("row", "col"),
            P("col", "row"),
            P(None, "row"),
            P("row", "col"),
            P("col", "row"),
            P("row", "col"),
            P("col", "row"),
            P(None, "row"),
            P(None, "row"),
            P("row", "col"),
            P("row", "col"),
            P("col", "row"),
            P("col", "row"),
            P("row", "col"),
            P("row", "col"),
            P("col", "row"),
            P("col", "row"),
        ),
        check_vma=False,
    )
```

profile of v0, /device:TPU:0, one launch (start us, length us, event | category | flops | bytes accessed | tf_op | source)
XLA Modules:
  0.0 313.3 jit_solution(11491301340539677173)
XLA Ops:
  10.9 12.8 %all_gather.21 = bf16[2048,192]{0,1:T(8,128)(2,1)S(1)} all-gather(bf16[1024,192]{0,1:T(8,128)(2,1)S(1)} %copy-done.13), channel_id=1, replica_groups=mesh['dp'=4,'row'=4,'col'=2] {'col'}, dimensions={0}, use_global_device_ids=true | all-gather | bytes 1179648 | tf_op jit(solution)/shard_map/all_gather | solution.py:201
  24.7 5.1 %all-to-all-start = ((bf16[4,512,192]{1,2,0:T(8,128)(2,1)}), bf16[4,512,192]{1,2,0:T(8,128)(2,1)S(1)}, u32[]{:S(2)}, u32[]{:S(2)}) async-start(bf16[4,512,192]{1,2,0:T(8,128)(2,1)} %bitcast.147), calls=%async_computation | async-start | bytes 1572864 | tf_op jit(solution)/shard_map/all_to_all | solution.py:198
  29.8 40.2 %all-gather = f32[4,192,4]{1,2,0:T(4,128)S(1)} all-gather(f32[1,192,4]{1,2,0:T(4,128)S(1)} %bitcast.167), channel_id=1, replica_groups=mesh['dp'=4,'row'=4,'col'=2] {'row'}, dimensions={0}, use_global_device_ids=true | all-gather | bytes 15360 | tf_op jit(solution)/shard_map/all_gather | solution.py:203
  71.1 8.4 %all_gather.24 = bf16[2048,192]{0,1:T(8,128)(2,1)S(1)} all-gather(bf16[1024,192]{0,1:T(8,128)(2,1)S(1)} %copy-done.11), channel_id=1, replica_groups=mesh['dp'=4,'row'=4,'col'=2] {'col'}, dimensions={0}, use_global_device_ids=true | all-gather | bytes 1179648 | tf_op jit(solution)/shard_map/all_gather | solution.py:202
  82.8 4.2 %all-to-all-start.2 = ((bf16[4,512,192]{1,2,0:T(8,128)(2,1)}), bf16[4,512,192]{1,2,0:T(8,128)(2,1)}, u32[]{:S(2)}, u32[]{:S(2)}) async-start(bf16[4,512,192]{1,2,0:T(8,128)(2,1)} %bitcast.146), calls=%async_computation.2 | async-start | bytes 1572864 | tf_op jit(solution)/shard_map/all_to_all | solution.py:198
  98.7 4.5 %all-to-all-done.2 = bf16[4,512,192]{1,2,0:T(8,128)(2,1)} async-done(((bf16[4,512,192]{1,2,0:T(8,128)(2,1)}), bf16[4,512,192]{1,2,0:T(8,128)(2,1)}, u32[]{:S(2)}, u32[]{:S(2)}) %all-to-all-start.2) | async-done | bytes 786464 | tf_op jit(solution)/shard_map/all_to_all | solution.py:198
  103.2 3.9 %convolution_bitcast_fusion = f32[512,1920]{1,0:T(8,128)S(1)} fusion(bf16[512,768]{0,1:T(8,128)(2,1)} %bitcast.31, bf16[768,4608]{1,0:T(8,128)(2,1)} %all-gather.3.cloned.1.call-done), kind=kOutput, calls=%fused_computation.12 | convolution fusion | flops 1509949440 | bytes 7667712 | tf_op jit(solution)/shard_map/dot_general | solution.py:121
  109.8 7.4 %fusion.1 = f32[6,512,512]{1,2,0:T(8,128)} fusion(pred[512,512]{0,1:T(8,128)(4,1)} %fusion.38, bf16[512,6,48]{0,2,1:T(8,128)(2,1)S(1)} %get-tuple-element.202, bf16[512,6,8]{0,2,1:T(8,128)(2,1)S(1)} %get-tuple-element.193, bf16[512,6,8]{0,2,1:T(8,128)(2,1)S(1)} %get-tuple-element.194, bf16[512,6,48]{0,2,1:T(8,128)(2,1)S(1)} %get-tuple-element.201, ...), kind=kOutput, calls=%fused_computation.3 | convolution fusion | flops 415239680 | bytes 7340032 | tf_op jit(solution)/shard_map/while/body/eval_jaxpr/reduce_sum | solution.py:98
  117.2 4.3 %multiply_reduce_fusion.4 = (f32[512,6]{0,1:T(8,128)S(1)}, bf16[6,64,512]{2,1,0:T(8,128)(2,1)}) fusion(bf16[512,6,64]{0,2,1:T(8,128)(2,1)S(1)} %bitcast.152, f32[6,512,512]{1,2,0:T(8,128)} %fusion.1, f32[1,512,6,3,64]{1,4,3,2,0:T(8,128)S(1)} %copy-done.8), kind=kOutput, calls=%fused_computation.92 | convolution fusion | flops 203879424 | bytes 7483392 | tf_op jit(solution)/shard_map/while/body/eval_jaxpr/hqk,khd->qhd/dot_general | solution.py:101
  132.3 6.0 %fusion.9 = (bf16[512,1536]{1,0:T(8,128)(2,1)S(1)}, bf16[512,1536]{1,0:T(8,128)(2,1)}) fusion(f32[512,1920]{1,0:T(8,128)} %copy-done.30, bf16[768,4608]{1,0:T(8,128)(2,1)} %all-gather.3.cloned.1.call-done, f32[512,768]{1,0:T(8,128)S(1)} %copy-done.2, f32[768]{0:T(1024)S(1)} %copy-done.41, f32[768]{0:T(1024)S(1)} %copy-done.40, f32[512]{0:T(512)S(1)} %copy-done.34, ...), kind=kOutput, calls=%fused_computation.17 | convolution fusion | flops 1220149248 | bytes 10233856 | tf_op jit(solution)/shard_map/dot_general | solution.py:121
  145.4 3.5 %fusion.13 = bf16[768,1920]{0,1:T(8,128)(2,1)S(1)} fusion(bf16[512,768]{0,1:T(8,128)(2,1)} %bitcast.31, bf16[512,1536]{1,0:T(8,128)(2,1)} %get-tuple-element.176, bf16[512,384]{1,0:T(8,128)(2,1)S(1)} %copy.202), kind=kOutput, calls=%fused_computation.23 | convolution fusion | flops 1515356160 | bytes 5701632 | tf_op jit(solution)/shard_map/dot_general | solution.py:125
  149.0 3.4 %pad_maximum_fusion = bf16[768,4608]{0,1:T(8,128)(2,1)} fusion(bf16[768,1920]{0,1:T(8,128)(2,1)S(1)} %fusion.13, bf16[768,1536]{0,1:T(8,128)(2,1)S(1)} %copy.216, bf16[768,1152]{0,1:T(8,128)(2,1)S(1)} %copy-done.1), kind=kLoop, calls=%fused_computation.1 | loop fusion | flops 21233664 | bytes 14155776 | tf_op jit(solution)/shard_map/concatenate | solution.py:154
  152.4 10.3 %copy.228 = bf16[768,4608]{1,0:T(8,128)(2,1)} copy(bf16[768,4608]{0,1:T(8,128)(2,1)} %pad_maximum_fusion) | data formatting | bytes 14155776
  164.0 3.2 %fusion.17 = f32[512,768]{1,0:T(8,128)S(1)} fusion(bf16[512,1536]{1,0:T(8,128)(2,1)S(1)} %copy-done.45, bf16[768,4608]{1,0:T(8,128)(2,1)} %all-gather.3.cloned.1.call-done), kind=kOutput, calls=%fused_computation.28 | convolution fusion | flops 1207959552 | bytes 5505024 | tf_op jit(solution)/shard_map/dot_general | solution.py:131
  167.3 3.5 %multiply_reduce_fusion.1 = (f32[768]{0:T(1024)S(1)}, f32[512]{0:T(512)S(1)}, f32[768]{0:T(1024)S(1)}, f32[768]{0:T(1024)S(1)}, f32[512]{0:T(512)S(1)}, /*index=5*/f32[768]{0:T(1024)S(1)}, f32[512,768]{1,0:T(8,128)S(1)}) fusion(f32[512,768]{1,0:T(8,128)S(1)} %copy-done.3, f32[512]{0:T(512)S(1)} %copy-done.34, f32[512]{0:T(512)S(1)} %copy-done.32, ...), kind=kOutput, calls=%fused_computation.42 | convolution fusion | flops 911470592 | bytes 7694336 | tf_op jit(solution)/shard_map/dot_general | solution.py:131
  172.4 3.5 %all-to-all-start.3 = ((bf16[4,512,192]{1,2,0:T(8,128)(2,1)}), bf16[4,512,192]{1,2,0:T(8,128)(2,1)S(1)}, u32[]{:S(2)}, u32[]{:S(2)}) async-start(bf16[4,512,192]{1,2,0:T(8,128)(2,1)} %bitcast.47), calls=%async_computation.3 | async-start | bytes 1572864 | tf_op jit(solution)/shard_map/all_to_all | solution.py:270
  175.9 4.6 %fusion.27 = bf16[512,768]{1,0:T(8,128)(2,1)S(1)} fusion(bf16[768,4608]{1,0:T(8,128)(2,1)} %all-gather.3.cloned.1.call-done, bf16[512,1536]{1,0:T(8,128)(2,1)} %get-tuple-element.176, bf16[512,384]{1,0:T(8,128)(2,1)S(1)} %copy.202), kind=kOutput, calls=%fused_computation.57 | convolution fusion | flops 1514274816 | bytes 5701632 | tf_op jit(solution)/shard_map/dot_general | solution.py:131
  181.7 11.4 %all-to-all-done.3 = bf16[4,512,192]{1,2,0:T(8,128)(2,1)S(1)} async-done(((bf16[4,512,192]{1,2,0:T(8,128)(2,1)}), bf16[4,512,192]{1,2,0:T(8,128)(2,1)S(1)}, u32[]{:S(2)}, u32[]{:S(2)}) %all-to-all-start.3) | async-done | bytes 786464 | tf_op jit(solution)/shard_map/all_to_all | solution.py:270
  193.0 3.7 %all-to-all-start.1 = ((bf16[4,512,192]{1,2,0:T(8,128)(2,1)}), bf16[4,512,192]{1,2,0:T(8,128)(2,1)S(1)}, u32[]{:S(2)}, u32[]{:S(2)}) async-start(bf16[4,512,192]{1,2,0:T(8,128)(2,1)} %bitcast.29), calls=%async_computation.1 | async-start | bytes 1572864 | tf_op jit(solution)/shard_map/all_to_all | solution.py:270
  201.6 57.2 %psum.7 = f32[4,768]{1,0:T(4,128)S(1)} all-reduce(f32[4,768]{1,0:T(4,128)S(1)} %pad_maximum_fusion.6), channel_id=1, replica_groups=mesh['dp'=4,'row'=4,'col'=2] {'dp','row','col'}, use_global_device_ids=true, to_apply=%region_12.13 | all-reduce | flops 3072 | bytes 24576 | tf_op jit(solution)/shard_map/psum | solution.py:283
  266.7 5.8 %collective-permute-done = bf16[1024,192]{0,1:T(8,128)(2,1)S(1)} collective-permute-done((bf16[1024,192]{0,1:T(8,128)(2,1)S(1)}, bf16[1024,192]{0,1:T(8,128)(2,1)S(1)}, u32[]{:S(2)}, u32[]{:S(2)}) %collective-permute-start) | collective-permute-done | bytes 393248 | tf_op jit(solution)/shard_map/ppermute | solution.py:277
  274.5 7.5 %all_gather.26 = bf16[192,1920]{1,0:T(8,128)(2,1)S(1)} all-gather(bf16[48,1920]{1,0:T(8,128)(2,1)S(1)} %slice.169), channel_id=1, replica_groups=mesh['dp'=4,'row'=4,'col'=2] {'dp'}, dimensions={0}, use_global_device_ids=true | all-gather | bytes 921600 | tf_op jit(solution)/shard_map/all_gather | solution.py:159
  282.1 7.8 %all_gather.27 = bf16[192,1536]{1,0:T(8,128)(2,1)S(1)} all-gather(bf16[48,1536]{1,0:T(8,128)(2,1)S(1)} %slice-done), channel_id=1, replica_groups=mesh['dp'=4,'row'=4,'col'=2] {'dp'}, dimensions={0}, use_global_device_ids=true | all-gather | bytes 737280 | tf_op jit(solution)/shard_map/all_gather | solution.py:159
  289.9 6.8 %all_gather.25 = bf16[192,1152]{1,0:T(8,128)(2,1)S(1)} all-gather(bf16[48,1152]{1,0:T(8,128)(2,1)S(1)} %slice-done.1), channel_id=1, replica_groups=mesh['dp'=4,'row'=4,'col'=2] {'dp'}, dimensions={0}, use_global_device_ids=true | all-gather | bytes 552960 | tf_op jit(solution)/shard_map/all_gather | solution.py:159
  (188 shorter events, 69.2 us)
Async XLA Ops:
  7.2 83.2 %all-gather.3.cloned.1.call-start = ((), (), s32[]{:S(2)}) async-start(), calls=%async_computation.5 | async-start | bytes 7520256 | tf_op jit(solution)/shard_map/all_gather | solution.py:150
  23.7 6.0 %copy-start.37 = (f32[4,192]{1,0:T(4,128)S(1)}, f32[4,192]{1,0:T(4,128)}, u32[]{:S(2)}) copy-start(f32[4,192]{1,0:T(4,128)} %param.21) | copy-start | bytes 9220
  23.7 46.3 %copy-start.39 = (s32[4,512]{1,0:T(4,128)S(1)}, s32[4,512]{1,0:T(4,128)}, u32[]{:S(2)}) copy-start(s32[4,512]{1,0:T(4,128)} %param.20) | copy-start | bytes 24580
  23.7 47.4 %copy-start.11 = (bf16[1024,192]{0,1:T(8,128)(2,1)S(1)}, bf16[1024,192]{0,1:T(8,128)(2,1)}, u32[]{:S(2)}) copy-start(bf16[1024,192]{0,1:T(8,128)(2,1)} %param.19) | copy-start | bytes 1179652
  24.7 58.1 %all-to-all-start = ((bf16[4,512,192]{1,2,0:T(8,128)(2,1)}), bf16[4,512,192]{1,2,0:T(8,128)(2,1)S(1)}, u32[]{:S(2)}, u32[]{:S(2)}) async-start(bf16[4,512,192]{1,2,0:T(8,128)(2,1)} %bitcast.147), calls=%async_computation | async-start | bytes 1572864 | tf_op jit(solution)/shard_map/all_to_all | solution.py:198
  71.1 23.4 %copy-start.35 = (f32[768]{0:T(1024)}, f32[768]{0:T(1024)S(1)}, u32[]{:S(2)}) copy-start(f32[768]{0:T(1024)S(1)} %get-tuple-element.150) | copy-start | bytes 9220
  82.8 20.4 %all-to-all-start.2 = ((bf16[4,512,192]{1,2,0:T(8,128)(2,1)}), bf16[4,512,192]{1,2,0:T(8,128)(2,1)}, u32[]{:S(2)}, u32[]{:S(2)}) async-start(bf16[4,512,192]{1,2,0:T(8,128)(2,1)} %bitcast.146), calls=%async_computation.2 | async-start | bytes 1572864 | tf_op jit(solution)/shard_map/all_to_all | solution.py:198
  87.0 186.5 %reduce-scatter.4.cloned.1.call-start = ((), (), s32[]{:S(2)}) async-start(), calls=%async_computation.6 | async-start | bytes 7520256
  89.2 5.3 %copy-start.31 = (f32[512]{0:T(512)}, f32[512]{0:T(512)S(1)}, u32[]{:S(2)}) copy-start(f32[512]{0:T(512)S(1)} %get-tuple-element.197) | copy-start | bytes 6148
  89.2 5.3 %copy-start.33 = (f32[512]{0:T(512)}, f32[512]{0:T(512)S(1)}, u32[]{:S(2)}) copy-start(f32[512]{0:T(512)S(1)} %get-tuple-element.198) | copy-start | bytes 6148
  109.8 7.4 %copy-start.8 = (f32[1,512,6,3,64]{1,4,3,2,0:T(8,128)S(1)}, f32[1,512,6,3,64]{1,4,3,2,0:T(8,128)}, u32[]{:S(2)}) copy-start(f32[1,512,6,3,64]{1,4,3,2,0:T(8,128)} %copy-done.7) | copy-start | bytes 7077892
  117.2 4.6 %copy-start = (f32[6,512,512]{1,2,0:T(8,128)S(1)}, f32[6,512,512]{1,2,0:T(8,128)}, u32[]{:S(2)}) copy-start(f32[6,512,512]{1,2,0:T(8,128)} %fusion.1) | copy-start | bytes 18874372
  172.4 20.6 %all-to-all-start.3 = ((bf16[4,512,192]{1,2,0:T(8,128)(2,1)}), bf16[4,512,192]{1,2,0:T(8,128)(2,1)S(1)}, u32[]{:S(2)}, u32[]{:S(2)}) async-start(bf16[4,512,192]{1,2,0:T(8,128)(2,1)} %bitcast.47), calls=%async_computation.3 | async-start | bytes 1572864 | tf_op jit(solution)/shard_map/all_to_all | solution.py:270
  193.0 65.7 %all-to-all-start.1 = ((bf16[4,512,192]{1,2,0:T(8,128)(2,1)}), bf16[4,512,192]{1,2,0:T(8,128)(2,1)S(1)}, u32[]{:S(2)}, u32[]{:S(2)}) async-start(bf16[4,512,192]{1,2,0:T(8,128)(2,1)} %bitcast.29), calls=%async_computation.1 | async-start | bytes 1572864 | tf_op jit(solution)/shard_map/all_to_all | solution.py:270
  199.6 65.1 %collective-permute-start.1 = (bf16[1024,192]{0,1:T(8,128)(2,1)S(1)}, bf16[1024,192]{0,1:T(8,128)(2,1)}, u32[]{:S(2)}, u32[]{:S(2)}) collective-permute-start(bf16[1024,192]{0,1:T(8,128)(2,1)S(1)} %bitcast.162), channel_id=1, source_target_pairs={{0,1},{1,0},{2,3},{3,2},{4,5},{5,4},{6,7},{7,6},{8,9},{9,8},{10,11... | collective-permute-start | bytes 1179656 | tf_op jit(solution)/shard_map/ppermute | solution.py:277
  259.9 4.0 %copy-start.38 = (f32[4,192]{1,0:T(4,128)S(1)}, f32[4,192]{1,0:T(4,128)}, u32[]{:S(2)}) copy-start(f32[4,192]{1,0:T(4,128)} %param.21) | copy-start | bytes 9220
  260.0 4.7 %copy-start.12 = (bf16[1024,192]{0,1:T(8,128)(2,1)S(1)}, bf16[1024,192]{0,1:T(8,128)(2,1)}, u32[]{:S(2)}) copy-start(bf16[1024,192]{0,1:T(8,128)(2,1)} %param.19) | copy-start | bytes 1179652
  261.4 11.1 %copy-start.14 = (bf16[1024,192]{0,1:T(8,128)(2,1)S(1)}, bf16[1024,192]{0,1:T(8,128)(2,1)}, u32[]{:S(2)}) copy-start(bf16[1024,192]{0,1:T(8,128)(2,1)} %param.18) | copy-start | bytes 1179652
  261.6 10.9 %collective-permute-start = (bf16[1024,192]{0,1:T(8,128)(2,1)S(1)}, bf16[1024,192]{0,1:T(8,128)(2,1)S(1)}, u32[]{:S(2)}, u32[]{:S(2)}) collective-permute-start(bf16[1024,192]{0,1:T(8,128)(2,1)S(1)} %bitcast.163), channel_id=1, source_target_pairs={{0,1},{1,0},{2,3},{3,2},{4,5},{5,4},{6,7},{7,6},{8,9},{9,8},{10,11... | collective-permute-start | bytes 1179656 | tf_op jit(solution)/shard_map/ppermute | solution.py:277
  274.5 7.6 %slice-start = ((bf16[48,4608]{1,0:T(8,128)(2,1)}), bf16[48,1536]{1,0:T(8,128)(2,1)S(1)}, s32[]{:S(2)}) async-start(bf16[48,4608]{1,0:T(8,128)(2,1)} %reduce-scatter.4.cloned.1.call-done), calls=%async_computation.7 | async-start | bytes 294912 | tf_op jit(solution)/shard_map/slice | solution.py:158
  274.5 15.4 %slice-start.1 = ((bf16[48,4608]{1,0:T(8,128)(2,1)}), bf16[48,1152]{1,0:T(8,128)(2,1)S(1)}, s32[]{:S(2)}) async-start(bf16[48,4608]{1,0:T(8,128)(2,1)} %reduce-scatter.4.cloned.1.call-done), calls=%async_computation.8 | async-start | bytes 221184 | tf_op jit(solution)/shard_map/slice | solution.py:158
  282.0 14.7 %copy-start.4 = (f32[1536,192]{0,1:T(8,128)S(1)}, f32[1536,192]{0,1:T(8,128)}, u32[]{:S(2)}) copy-start(f32[1536,192]{0,1:T(8,128)} %param.25) | copy-start | bytes 3538948
  282.0 14.7 %copy-start.15 = (f32[1536,192]{0,1:T(8,128)S(1)}, f32[1536,192]{0,1:T(8,128)}, u32[]{:S(2)}) copy-start(f32[1536,192]{0,1:T(8,128)} %param.34) | copy-start | bytes 3538948
  282.0 14.7 %copy-start.16 = (f32[1536,192]{0,1:T(8,128)S(1)}, f32[1536,192]{0,1:T(8,128)}, u32[]{:S(2)}) copy-start(f32[1536,192]{0,1:T(8,128)} %param.35) | copy-start | bytes 3538948
  (32 other events, 77.7 us)
Sparse Core Ops, SparseCore 0:
  10.9 76.4 all-gather.2
  162.8 102.5 reduce-scatter.3
where the time goes:
time: 317 us; the launch traced here: 313 us
  blocking collectives  141 us (44%)
  matrix products  47.2 us (15%)
  local copies, waits for them, and re-layouts  42.1 us (13%)
  other arithmetic  25.5 us (8%)
  waiting for transfers between devices  21.7 us (7%)
  starting transfers between devices  21 us (7%)
  between operations  15.2 us (5%)
    psum x1, blocking collectives, on_device(): lax.psum(norm_part, ('dp', 'row', 'col'))  57.2 us
    all_gather x1, blocking collectives, on_device(): norm_full = lax.all_gather(norm_params, 'row', axis=1, tiled=True)  40.2 us
    all_gather x3, blocking collectives, reduce_weights(): lax.all_gather(piece, 'dp', axis=0, tiled=True).astype(jnp.float32)  22.1 us
    unnamed x96, local copies, waits for them, and re-layouts  21 us
    all_gather x1, blocking collectives, on_device(): x16 = to_tokens(lax.all_gather(tokens_in, 'col', axis=0, tiled=True))  12.8 us
    dot_general x3, matrix products, dot32(): return jnp.dot(left, right, preferred_element_type=jnp.float32)  12.5 us
    all_to_all x2, waiting for transfers between devices, to_features(): blocks = lax.all_to_all(jnp.moveaxis(blocks, 1, 0), 'row', 0, 0, tiled=True)  11.4 us
    dot_general x3, matrix products, dot_cols(): lax.dot_general(left, right, (((1,), (1,)), ((), ())), preferred_element_...  11.3 us
  transfers between devices with their start and end apart: 8, of which 3 were waited for; matrix products, arithmetic and copies ran while one was open for 12% of the time, Pallas kernels for 0%

commit v1 on v0

v1 whole, which is shorter than its diff:
```python
import functools
import math

import jax
import jax.numpy as jnp
from jax import lax
from jax.experimental import pallas as pl
from jax.experimental.pallas import tpu as pltpu
from jax.sharding import PartitionSpec as P

D = 768
HEAD_DIM = 64
ROT_DIM = 16
SEQ_LEN = 512
STEP = 3


norm_eps = 1e-05
rotary_base = 10000.0
learn_rate = 0.01
beta_first = 0.9
beta_second = 0.95
adam_eps = 1e-08
decay_rate = 0.1
mask_fill = -1e30
inv_sqrt_two = 0.7071067811865476
inv_sqrt_two_pi = 0.3989422804014327


def adam_update(weight, first, second, grad, decay):
    first_new = beta_first * first + (1.0 - beta_first) * grad
    second_new = beta_second * second + (1.0 - beta_second) * grad * grad
    first_hat = first_new / (1.0 - beta_first**STEP)
    second_hat = second_new / (1.0 - beta_second**STEP)
    weight_new = weight - learn_rate * (
        first_hat / (jnp.sqrt(second_hat) + adam_eps) + decay * weight
    )
    return (weight_new, first_new, second_new)


MESH = pl.DeviceIdType.MESH
LANES = 128
QUARTERS = 4
WINDOW = 256
QBLOCK = 128


def remote(src, dst, send_sem, recv_sem, device):
    return pltpu.make_async_remote_copy(
        src_ref=src,
        dst_ref=dst,
        send_sem=send_sem,
        recv_sem=recv_sem,
        device_id=device,
        device_id_type=MESH,
    )


def places(row_count):
    data, row, col = lax.axis_index("dp"), lax.axis_index("row"), lax.axis_index("col")
    quarter = lax.rem(data, QUARTERS)
    far = data - quarter + lax.rem(quarter + 2, QUARTERS)
    mate = data + 1 - 2 * lax.rem(quarter, 2)
    return data, row, col, quarter, far, mate


def greet(peers):
    barrier = pltpu.get_barrier_semaphore()
    for peer in peers:
        pl.semaphore_signal(barrier, inc=1, device_id=peer, device_id_type=MESH)
    pl.semaphore_wait(barrier, len(peers))


def gather_kernel(row_count, tok, cot, nrm, w0, w1, w2, xg, cg, ng, g0, g1, g2, hop, *sems):
    (nrm_s, nrm_r, x_s, x_r, xy_s, xy_r, h_s, h_r, c_s, c_r, cy_s, cy_r, loc,
     z_s, z_r, f_s, f_r, m_s, m_r) = sems
    data, row, col, quarter, far, mate = places(row_count)
    shares = tok.shape[0]
    other = 1 - col
    home = row // shares
    own_w, all_w = (w0, w1, w2), (g0, g1, g2)
    groups = len(own_w)
    depth = w0.shape[0] // QUARTERS
    others = [lax.rem(row + k, row_count) for k in range(1, row_count)]
    greet(
        [(data, t, col) for t in others]
        + [(data, row, other), (far, row, col), (mate, row, col)]
    )

    def rows(part):
        return pl.ds(pl.multiple_of(part * depth, depth), depth)

    def step_copy(g, src, up):
        at = all_w[g].at[src, rows(quarter)]
        return remote(at, at, z_s.at[int(up), g, src], z_r.at[g, src],
                      (data, row + 1 if up else row - 1, col))

    def own_copy(g, up):
        return remote(own_w[g].at[rows(quarter)], all_w[g].at[row, rows(quarter)],
                      z_s.at[int(up), g, row], z_r.at[g, row],
                      (data, row + 1 if up else row - 1, col))

    def far_copy(g, src):
        at = all_w[g].at[src, rows(quarter)]
        return remote(at, at, f_s.at[g, src], f_r.at[g, src], (far, row, col))

    def far_wait(g, src):
        at = all_w[g].at[src, rows(lax.rem(quarter + 2, QUARTERS))]
        remote(at, at, f_s.at[g, src], f_r.at[g, src], (far, row, col)).wait_recv()

    def mate_copy(g, src, second):
        part = lax.rem(quarter + 2, QUARTERS) if second else quarter
        at = all_w[g].at[src, rows(part)]
        return remote(at, at, m_s.at[int(second), g, src], m_r.at[int(second), g, src],
                      (mate, row, col))

    def mate_wait(g, src, second):
        theirs = quarter + 1 - 2 * lax.rem(quarter, 2)
        part = lax.rem(theirs + 2, QUARTERS) if second else theirs
        at = all_w[g].at[src, rows(part)]
        remote(at, at, m_s.at[int(second), g, src], m_r.at[int(second), g, src],
               (mate, row, col)).wait_recv()

    def norm_copy(k):
        return remote(nrm, ng.at[row], nrm_s.at[k], nrm_r.at[row], (data, others[k], col))

    def norm_wait(k):
        remote(nrm, ng.at[others[k]], nrm_s.at[k], nrm_r.at[others[k]],
               (data, others[k], col)).wait_recv()

    def token_copy(j):
        return remote(tok.at[j], xg.at[row], x_s.at[j], x_r.at[row],
                      (data, col * shares + j, col))

    def token_local(j):
        return pltpu.make_async_copy(tok.at[j], xg.at[row], loc.at[0])

    def hop_copy(j):
        return remote(cot.at[j], hop.at[j], h_s.at[j], h_r.at[j], (data, row, other))

    def cot_copy(j):
        return remote(hop.at[j], cg.at[row], c_s.at[j], c_r.at[row],
                      (data, other * shares + j, col))

    def cot_local(j):
        return pltpu.make_async_copy(hop.at[j], cg.at[row], loc.at[1])

    def x_wait(src):
        remote(tok.at[0], xg.at[src], x_s.at[0], x_r.at[src], (data, src, col)).wait_recv()

    def c_wait(src):
        remote(tok.at[0], cg.at[src], c_s.at[0], c_r.at[src], (data, src, col)).wait_recv()

    def across(ref, sems_, src):
        return remote(ref.at[src], ref.at[src], sems_[0].at[src], sems_[1].at[src],
                      (data, row, other))

    x_main = col == home
    c_main = col != home

    for k in range(row_count - 1):
        norm_copy(k).start()
    own_norm = pltpu.make_async_copy(nrm, ng.at[row], loc.at[2])
    own_norm.start()
    for j in range(shares):
        @pl.when(col * shares + j != row)
        def _():
            token_copy(j).start()

        @pl.when(col * shares + j == row)
        def _():
            token_local(j).start()
        hop_copy(j).start()

    def send_own(g):
        @pl.when(row + 1 < row_count)
        def _():
            own_copy(g, True).start()

        @pl.when(row > 0)
        def _():
            own_copy(g, False).start()

    pending = []

    def settle():
        for g, k, below in pending:
            src = row - k if below else row + k

            @pl.when(src >= 0 if below else src < row_count)
            def _():
                far_wait(g, src)
                mate_copy(g, src, True).start()
        pending.clear()

    def relay(g):
        for k in range(1, row_count):
            now = []
            for below in (True, False):
                src = row - k if below else row + k

                @pl.when(src >= 0 if below else src < row_count)
                def _():
                    step_copy(g, src, below).wait_recv()
                    onward = row + 1 < row_count if below else row > 0

                    @pl.when(onward)
                    def _():
                        step_copy(g, src, below).start()
                    far_copy(g, src).start()
                    mate_copy(g, src, False).start()
                now.append((g, k, below))
            settle()
            pending.extend(now)

    send_own(0)
    send_own(1)
    for j in range(shares):
        hop_copy(j).wait_recv()

        @pl.when(other * shares + j != row)
        def _():
            cot_copy(j).start()

        @pl.when(other * shares + j == row)
        def _():
            cot_local(j).start()

    @pl.when(x_main)
    def _():
        token_local(0).wait()
        across(xg, (xy_s, xy_r), row).start()
        for src in others:
            x_wait(src)
            across(xg, (xy_s, xy_r), src).start()

    relay(0)
    send_own(2)

    @pl.when(c_main)
    def _():
        cot_local(0).wait()
        across(cg, (cy_s, cy_r), row).start()
        for src in others:
            c_wait(src)
            across(cg, (cy_s, cy_r), src).start()

    for g in range(1, groups):
        relay(g)
    settle()

    for main, ref, pair in ((x_main, xg, (xy_s, xy_r)), (c_main, cg, (cy_s, cy_r))):
        @pl.when(main)
        def _():
            for src in range(row_count):
                across(ref, pair, src).wait_send()

        @pl.when(jnp.logical_not(main))
        def _():
            for src in range(row_count):
                across(ref, pair, src).wait_recv()
    own_norm.wait()
    for k in range(row_count - 1):
        norm_copy(k).wait_send()
        norm_wait(k)
    for j in range(shares):
        @pl.when(col * shares + j != row)
        def _():
            token_copy(j).wait_send()

        @pl.when(other * shares + j != row)
        def _():
            cot_copy(j).wait_send()
        hop_copy(j).wait_send()
    for g in range(groups):
        @pl.when(row + 1 < row_count)
        def _():
            own_copy(g, True).wait_send()

        @pl.when(row > 0)
        def _():
            own_copy(g, False).wait_send()
        for k in range(1, row_count):
            for below in (True, False):
                src = row - k if below else row + k

                @pl.when(src >= 0 if below else src < row_count)
                def _():
                    onward = row + 1 < row_count if below else row > 0

                    @pl.when(onward)
                    def _():
                        step_copy(g, src, below).wait_send()
                    far_copy(g, src).wait_send()
                    for second in (False, True):
                        mate_copy(g, src, second).wait_send()
                        mate_wait(g, src, second)


def gather_all(row_count, tok, cot, nrm, weights):
    shares, packed, _ = tok.shape
    bf16 = jnp.bfloat16
    groups = len(weights)
    dma = pltpu.SemaphoreType.DMA
    anywhere = pl.BlockSpec(memory_space=pl.ANY)
    vmem = pl.BlockSpec(memory_space=pltpu.VMEM)
    n = row_count
    sent = sum(w.size for w in weights) * 2 + tok.size * 8
    return pl.pallas_call(
        functools.partial(gather_kernel, row_count),
        out_shape=[
            jax.ShapeDtypeStruct((n, packed, LANES), bf16),
            jax.ShapeDtypeStruct((n, packed, LANES), bf16),
            jax.ShapeDtypeStruct((n,) + nrm.shape, jnp.float32),
        ] + [jax.ShapeDtypeStruct((n,) + w.shape, bf16) for w in weights],
        in_specs=[anywhere] * (3 + groups),
        out_specs=[vmem] * 3 + [anywhere] * groups,
        scratch_shapes=[
            pltpu.VMEM(tok.shape, bf16),
            dma((n,)), dma((n,)),
            dma((shares,)), dma((n,)), dma((n,)), dma((n,)),
            dma((shares,)), dma((shares,)),
            dma((shares,)), dma((n,)), dma((n,)), dma((n,)),
            dma((3,)),
            dma((2, groups, n)), dma((groups, n)),
            dma((groups, n)), dma((groups, n)),
            dma((2, groups, n)), dma((2, groups, n)),
        ],
        compiler_params=pltpu.CompilerParams(
            collective_id=0, has_side_effects=True, vmem_limit_bytes=16 << 20
        ),
        cost_estimate=pl.CostEstimate(flops=0, bytes_accessed=sent, transcendentals=0),
        name="gather",
    )(tok, cot, nrm, *weights)


def reduce_kernel(row_count, groups_out, outp, gradp, nrmp, p0, p1, p2,
                  out_t, grad_t, nrm_t, r0, r1, r2, *scratch):
    (oy, od, gy, gd, gh, nz, nc, nd, nrm1, nrm2,
     c0, c1, c2, fs0, fs1, fs2, fr0, fr1, fr2, zs0, zs1, zs2, zr0, zr1, zr2, ex0, ex1, ex2,
     oy_s, oy_r, oz_s, oz_r, gy_s, gy_r, gz_s, gz_r, gh_s, gh_r,
     nz_s, nz_r, nc_s, nc_r, nd_s, nd_r,
     c_s, c_r, f_s, f_r, z_s, z_r, e_s, e_r, a_s, a_r, b_s, b_r, loc) = scratch
    data, row, col, quarter, far, mate = places(row_count)
    parts, total = (p0, p1, p2), (r0, r1, r2)
    crecv, fsend, frecv = (c0, c1, c2), (fs0, fs1, fs2), (fr0, fr1, fr2)
    zsend, zrecv, extra = (zs0, zs1, zs2), (zr0, zr1, zr2), (ex0, ex1, ex2)
    groups = len(parts)
    shares = out_t.shape[0]
    other = 1 - col
    home = row // shares
    depth = parts[0].shape[1] // QUARTERS
    data_count = QUARTERS * groups_out
    others = [lax.rem(row + k, row_count) for k in range(1, row_count)]
    order = others + [row]
    wider = [lax.rem(data + QUARTERS * k, data_count) for k in range(1, groups_out)]
    everyone = [lax.rem(data + k, data_count) for k in range(1, data_count)]
    greet([(data, t, col) for t in others] + [(data, row, other)]
          + [(t, row, col) for t in everyone])
    f32, bf16 = jnp.float32, jnp.bfloat16
    half = lax.rem(quarter + 2, QUARTERS)
    theirs = quarter + 1 - 2 * lax.rem(quarter, 2)
    theirs_half = lax.rem(theirs + 2, QUARTERS)

    def rows(part):
        return pl.ds(pl.multiple_of(part * depth, depth), depth)

    def norm_z(k):
        return remote(nrmp.at[others[k]], nz.at[row], nz_s.at[k], nz_r.at[row],
                      (data, others[k], col))

    def norm_z_wait(k):
        remote(nrmp.at[0], nz.at[others[k]], nz_s.at[k], nz_r.at[others[k]],
               (data, others[k], col)).wait_recv()

    def norm_c():
        return remote(nrm1, nc, nc_s, nc_r, (data, row, other))

    def norm_d(k):
        return remote(nrm2, nd.at[data], nd_s.at[k], nd_r.at[data], (everyone[k], row, col))

    def norm_d_wait(k):
        remote(nrm2, nd.at[everyone[k]], nd_s.at[k], nd_r.at[everyone[k]],
               (everyone[k], row, col)).wait_recv()

    def out_y(t):
        return remote(outp.at[t], oy.at[t], oy_s.at[t], oy_r.at[t], (data, row, other))

    def grad_y(t):
        return remote(gradp.at[t], gy.at[t], gy_s.at[t], gy_r.at[t], (data, row, other))

    slot = row - home * shares

    def out_z(t):
        return remote(od.at[t], out_t.at[slot], oz_s.at[t], oz_r.at[slot], (data, t, col))

    def out_z_wait(j):
        remote(od.at[0], out_t.at[j], oz_s.at[0], oz_r.at[j], (data, row, col)).wait_recv()

    def grad_z(t):
        return remote(gd.at[t], gh.at[slot], gz_s.at[t], gz_r.at[slot], (data, t, col))

    def grad_z_wait(j):
        remote(gd.at[0], gh.at[j], gz_s.at[0], gz_r.at[j], (data, row, col)).wait_recv()

    def grad_h(j):
        return remote(gh.at[j], grad_t.at[j], gh_s.at[j], gh_r.at[j], (data, row, other))

    def mate_part(g, t, second):
        part = theirs_half if second else theirs
        return remote(parts[g].at[t, rows(part)], crecv[g].at[int(second), t],
                      c_s.at[int(second), g, t], c_r.at[int(second), g, t], (mate, row, col))

    def far_part(g, t):
        return remote(fsend[g].at[t], frecv[g].at[t], f_s.at[g, t], f_r.at[g, t],
                      (far, row, col))

    def row_part(g, t):
        return remote(zsend[g].at[t], zrecv[g].at[row], z_s.at[g, t], z_r.at[g, row],
                      (data, t, col))

    def row_wait(g, src):
        remote(zsend[g].at[src], zrecv[g].at[src], z_s.at[g, src], z_r.at[g, src],
               (data, src, col)).wait_recv()

    def wide_part(g, k):
        return remote(total[g].at[rows(quarter)], extra[g].at[data // QUARTERS],
                      e_s.at[g, k], e_r.at[g, data // QUARTERS], (wider[k], row, col))

    def wide_wait(g, k):
        remote(total[g].at[rows(quarter)], extra[g].at[wider[k] // QUARTERS],
               e_s.at[g, k], e_r.at[g, wider[k] // QUARTERS], (wider[k], row, col)).wait_recv()

    def far_sum(g):
        at = total[g].at[rows(quarter)]
        return remote(at, at, a_s.at[g], a_r.at[g], (far, row, col))

    def far_sum_wait(g):
        at = total[g].at[rows(half)]
        remote(at, at, a_s.at[g], a_r.at[g], (far, row, col)).wait_recv()

    def mate_sum(g, second):
        at = total[g].at[rows(half if second else quarter)]
        return remote(at, at, b_s.at[int(second), g], b_r.at[int(second), g], (mate, row, col))

    def mate_sum_wait(g, second):
        at = total[g].at[rows(theirs_half if second else theirs)]
        remote(at, at, b_s.at[int(second), g], b_r.at[int(second), g],
               (mate, row, col)).wait_recv()

    o_main = col == home
    g_main = col != home

    for k in range(row_count - 1):
        norm_z(k).start()

    @pl.when(jnp.logical_not(o_main))
    def _():
        for t in order:
            out_y(t).start()

    @pl.when(jnp.logical_not(g_main))
    def _():
        for t in order:
            grad_y(t).start()
    for g in range(groups):
        for t in order:
            mate_part(g, t, True).start()
        for t in order:
            mate_part(g, t, False).start()

    def stage_far(g, t):
        mate_part(g, t, True).wait_recv()
        own = parts[g][t, rows(half), :].astype(f32)
        fsend[g][t] = (own + crecv[g][1, t].astype(f32)).astype(bf16)
        far_part(g, t).start()

    def stage_row(g, t, own_row):
        mate_part(g, t, False).wait_recv()
        far_part(g, t).wait_recv()
        mine = parts[g][t, rows(quarter), :].astype(f32)
        mine = mine + crecv[g][0, t].astype(f32) + frecv[g][t].astype(f32)
        zsend[g][t] = mine.astype(bf16)
        if not own_row:
            row_part(g, t).start()

    def outputs_out():
        @pl.when(o_main)
        def _():
            for t in order:
                out_y(t).wait_recv()
                od[t] = (outp[t].astype(f32) + oy[t].astype(f32)).astype(bf16)
                if t is row:
                    pltpu.make_async_copy(od.at[t], out_t.at[slot], loc.at[0]).start()
                else:
                    out_z(t).start()

    def outputs_grad():
        @pl.when(g_main)
        def _():
            for t in order:
                grad_y(t).wait_recv()
                gd[t] = (gradp[t].astype(f32) + gy[t].astype(f32)).astype(bf16)
                if t is row:
                    pltpu.make_async_copy(gd.at[t], gh.at[slot], loc.at[1]).start()
                else:
                    grad_z(t).start()

    def grads_home():
        for j in range(shares):
            @pl.when(other * shares + j != row)
            def _():
                grad_z_wait(j)

            @pl.when(other * shares + j == row)
            def _():
                pltpu.make_async_copy(gd.at[row], gh.at[slot], loc.at[1]).wait()
            grad_h(j).start()

    def finish(g):
        acc = zsend[g][row].astype(f32)
        for src in others:
            row_wait(g, src)
            acc = acc + zrecv[g][src].astype(f32)
        total[g][rows(quarter), :] = acc.astype(bf16)
        if wider:
            for k in range(len(wider)):
                wide_part(g, k).start()
            for k in range(len(wider)):
                wide_wait(g, k)
                acc = acc + extra[g][wider[k] // QUARTERS].astype(f32)
            for k in range(len(wider)):
                wide_part(g, k).wait_send()
            total[g][rows(quarter), :] = acc.astype(bf16)
        far_sum(g).start()
        mate_sum(g, False).start()

    pieces = [(g, t) for g in range(groups) for t in order]
    lag = 2
    for n in range(len(pieces) + lag):
        if n < len(pieces):
            stage_far(*pieces[n])
        if n == 1:
            outputs_out()
        if n == 3:
            outputs_grad()
            acc = nrmp[row]
            for k in range(row_count - 1):
                norm_z_wait(k)
                acc = acc + nz[others[k]]
            nrm1[...] = acc
            norm_c().start()
        if n == 6:
            norm_c().wait_recv()
            nrm2[...] = nrm1[...] + nc[...]
            for k in range(len(everyone)):
                norm_d(k).start()
        if n == 8:
            grads_home()
        if n >= lag:
            g, t = pieces[n - lag]
            stage_row(g, t, t is row)
            if (n - lag) % row_count == row_count - 1 and g > 0:
                finish(g - 1)
    finish(groups - 1)
    acc = nrm2[...]
    for k in range(len(everyone)):
        norm_d_wait(k)
        acc = acc + nd[everyone[k]]
    nrm_t[...] = acc
    for g in range(groups):
        far_sum_wait(g)
        mate_sum(g, True).start()

    @pl.when(jnp.logical_not(o_main))
    def _():
        for t in range(row_count):
            out_y(t).wait_send()

    @pl.when(jnp.logical_not(g_main))
    def _():
        for t in range(row_count):
            grad_y(t).wait_send()

    @pl.when(o_main)
    def _():
        pltpu.make_async_copy(od.at[row], out_t.at[slot], loc.at[0]).wait()
        for t in others:
            out_z(t).wait_send()

    @pl.when(g_main)
    def _():
        for t in others:
            grad_z(t).wait_send()
    for j in range(shares):
        @pl.when(col * shares + j != row)
        def _():
            out_z_wait(j)
        grad_h(j).wait()
    for k in range(row_count - 1):
        norm_z(k).wait_send()
    norm_c().wait_send()
    for k in range(len(everyone)):
        norm_d(k).wait_send()
    for g in range(groups):
        for t in range(row_count):
            for second in (False, True):
                mate_part(g, t, second).wait_send()
            far_part(g, t).wait_send()
        for t in others:
            row_part(g, t).wait_send()
        far_sum(g).wait_send()
        for second in (False, True):
            mate_sum(g, second).wait_send()
            mate_sum_wait(g, second)


def reduce_all(row_count, data_count, shares, outp, gradp, nrmp, parts):
    n = row_count
    bf16, f32 = jnp.bfloat16, jnp.float32
    dma = pltpu.SemaphoreType.DMA
    vmem = pl.BlockSpec(memory_space=pltpu.VMEM)
    groups = len(parts)
    groups_out = data_count // QUARTERS
    block = outp.shape[1:]
    small = nrmp.shape[1:]
    depth = parts[0].shape[1] // QUARTERS
    widths = [p.shape[2] for p in parts]

    def each(lead, dtype=bf16):
        return [pltpu.VMEM(lead + (depth, w), dtype) for w in widths]

    return pl.pallas_call(
        functools.partial(reduce_kernel, row_count, groups_out),
        out_shape=[
            jax.ShapeDtypeStruct((shares,) + block, bf16),
            jax.ShapeDtypeStruct((shares,) + block, bf16),
            jax.ShapeDtypeStruct(small, f32),
        ] + [jax.ShapeDtypeStruct((p.shape[1], p.shape[2]), bf16) for p in parts],
        in_specs=[vmem] * (3 + groups),
        out_specs=[vmem] * (3 + groups),
        scratch_shapes=[
            pltpu.VMEM((n,) + block, bf16), pltpu.VMEM((n,) + block, bf16),
            pltpu.VMEM((n,) + block, bf16), pltpu.VMEM((n,) + block, bf16),
            pltpu.VMEM((shares,) + block, bf16),
            pltpu.VMEM((n,) + small, f32), pltpu.VMEM(small, f32),
            pltpu.VMEM((data_count,) + small, f32),
            pltpu.VMEM(small, f32), pltpu.VMEM(small, f32),
            *each((2, n)), *each((n,)), *each((n,)), *each((n,)), *each((n,)),
            *each((groups_out,)),
            dma((n,)), dma((n,)), dma((n,)), dma((shares,)),
            dma((n,)), dma((n,)), dma((n,)), dma((shares,)), dma((shares,)), dma((shares,)),
            dma((n,)), dma((n,)), dma, dma, dma((data_count,)), dma((data_count,)),
            dma((2, groups, n)), dma((2, groups, n)),
            dma((groups, n)), dma((groups, n)),
            dma((groups, n)), dma((groups, n)),
            dma((groups, groups_out)), dma((groups, groups_out)),
            dma((groups,)), dma((groups,)),
            dma((2, groups)), dma((2, groups)), dma((2,)),
        ],
        compiler_params=pltpu.CompilerParams(
            collective_id=1, has_side_effects=True, vmem_limit_bytes=44 << 20
        ),
        cost_estimate=pl.CostEstimate(flops=0, bytes_accessed=1 << 24, transcendentals=0),
        name="reduce",
    )(outp, gradp, nrmp, *parts)


def lane_low(shape):
    return lax.broadcasted_iota(jnp.int32, shape, len(shape) - 1) < HEAD_DIM


def swap(tile):
    return pltpu.roll(tile, HEAD_DIM, 1)


def compute_kernel(row_count, width, seg_ref, freq_ref, xg, cg, ng, w0, w1, w2, a0, a1, a2,
                   outp, gradp, nrmp, gq, gu, go,
                   wq, wu, wo, normed, fi, si, co, fit, sit, cot, dcat, act, hg, pg, comb,
                   dk, dv, sem):
    f32, bf16 = jnp.float32, jnp.bfloat16
    row = lax.axis_index("row")
    length = xg.shape[1] * 2 // 3
    halflen = length // 2
    attn = wq.shape[1] // 3
    hidden = wu.shape[1]
    tail = row_count * LANES
    small = w0.shape[0] - LANES

    def loads(g, src, mine):
        own, gathered, dest = ((w0, a0, wq), (w1, a1, wu), (w2, a2, wo))[g]
        view = own if mine else gathered.at[src]
        return (
            pltpu.make_async_copy(view.at[pl.ds(0, LANES)],
                                  dest.at[pl.ds(src * LANES, LANES)], sem.at[0, g, src]),
            pltpu.make_async_copy(view.at[pl.ds(LANES, small)],
                                  dest.at[pl.ds(tail + src * small, small)], sem.at[1, g, src]),
        )

    for g in (0, 2, 1):
        for src in range(row_count):
            @pl.when(row == src)
            def _():
                for copy in loads(g, src, True):
                    copy.start()

            @pl.when(row != src)
            def _():
                for copy in loads(g, src, False):
                    copy.start()

    def landed(g):
        for src in range(row_count):
            for copy in loads(g, src, False):
                copy.wait()

    low = lane_low((halflen, LANES))

    def tails(ref, pair):
        left = ref[2 * pair, length:, :].astype(f32)
        right = ref[2 * pair + 1, length:, :].astype(f32)
        return jnp.concatenate(
            [jnp.where(low, left, swap(right)), jnp.where(low, swap(left), right)], 0)

    def tiles(ref):
        return [ref[r, :length, :].astype(f32) for r in range(row_count)] + [
            tails(ref, p) for p in range(row_count // 2)]

    xt = tiles(xg)
    mean = sum(jnp.sum(t, 1, keepdims=True) for t in xt) / width
    spread = sum(jnp.sum(t * t, 1, keepdims=True) for t in xt) / width - mean * mean
    rstd = lax.rsqrt(spread + norm_eps)
    low8 = lane_low((8, LANES))

    def norm_tile(n):
        if n < row_count:
            return ng[n, :, :LANES]
        left, right = ng[2 * (n - row_count), :, LANES:], ng[2 * (n - row_count) + 1, :, LANES:]
        return jnp.where(low8, left, swap(right))

    ct = tiles(cg)
    for n in range(len(xt)):
        at = slice(n * LANES, (n + 1) * LANES)
        gain = norm_tile(n)
        value = (xt[n] - mean) * rstd
        normed[:, at] = value
        first = (value * gain[0:1] + gain[1:2]).astype(bf16)
        second = (value * gain[2:3] + gain[3:4]).astype(bf16)
        cotan = ct[n].astype(bf16)
        fi[:, at] = first
        si[:, at] = second
        co[:, at] = cotan
        fit[at, :] = first.T
        sit[at, :] = second.T
        cot[at, :] = cotan.T

    def mm(a, b):
        return jnp.dot(a, b, preferred_element_type=f32)

    def mm_cols(a, b):
        return lax.dot_general(a, b, (((1,), (1,)), ((), ())), preferred_element_type=f32)

    def mm_rows(a, b):
        return lax.dot_general(a, b, (((0,), (0,)), ((), ())), preferred_element_type=f32)

    seg_row = seg_ref[pl.ds(row, 1), :].astype(f32)
    seg_col = jnp.broadcast_to(seg_row, (8, length)).T[:, 0:1]
    spans = []
    pos = []
    for i in range(length // QBLOCK):
        lo = max(0, i * QBLOCK - WINDOW)
        hi = (i + 1) * QBLOCK
        spans.append((i * QBLOCK, lo, hi))
    masks = []
    for at, lo, hi in spans:
        shape = (QBLOCK, hi - lo)
        qi = lax.broadcasted_iota(jnp.int32, shape, 0) + at
        ki = lax.broadcasted_iota(jnp.int32, shape, 1) + lo
        allowed = (seg_col[at:hi] == seg_row[:, lo:hi]) & (ki <= qi)
        masks.append(allowed)
        pos.append(jnp.sum(jnp.where(allowed, 1.0, 0.0), 1, keepdims=True) - 1.0)
    angle = jnp.concatenate(pos, 0) * freq_ref[0:1, :]
    cosine = jnp.cos(angle)
    sine = jnp.sin(angle)
    lane = lax.rem(lax.broadcasted_iota(jnp.int32, (length, LANES), 1), HEAD_DIM)
    half = ROT_DIM // 2
    up = jnp.where(lane < half, -sine, 0.0)
    down = jnp.where((lane >= half) & (lane < ROT_DIM), sine, 0.0)

    def turn(tile, sign):
        return (tile * cosine + sign * (pltpu.roll(tile, LANES - half, 1) * up
                                        + pltpu.roll(tile, half, 1) * down))

    landed(0)
    landed(2)
    dcat[...] = mm(co[...], wo[:, :attn]).astype(bf16)
    lowq = lane_low((length, LANES))
    lowb = lane_low((QBLOCK, LANES))
    scale = 1.0 / math.sqrt(HEAD_DIM)

    def pair_step(p, carry):
        at = pl.multiple_of(p * 3 * LANES, 3 * LANES)
        out_at = pl.ds(pl.multiple_of(p * LANES, LANES), LANES)
        packed = mm(fi[...], wq[:, pl.ds(at, 3 * LANES)])
        t0, t1, t2 = (packed[:, n * LANES:(n + 1) * LANES] for n in range(3))
        query = turn(jnp.where(lowq, t0, t1), 1.0).astype(bf16)
        keys = turn(swap(jnp.where(lowq, t2, t0)), 1.0).astype(bf16)
        values = jnp.where(lowq, t1, t2).astype(bf16)
        grads = dcat[:, out_at]
        dk[...] = jnp.zeros_like(dk)
        dv[...] = jnp.zeros_like(dv)
        zero = jnp.zeros((), bf16)
        dqs = []
        for (at_q, lo, hi), allowed in zip(spans, masks):
            qb = query[at_q:hi]
            gb = grads[at_q:hi]
            kw, vw = keys[lo:hi], values[lo:hi]
            mixed, dq, keep = [], [], []
            for head in range(2):
                sel = lowb if head == 0 else jnp.logical_not(lowb)
                qm = jnp.where(sel, qb, zero)
                gm = jnp.where(sel, gb, zero)
                scores = jnp.where(allowed, mm_cols(qm, kw) * scale, mask_fill)
                logsum = jnp.log(jnp.sum(jnp.exp(scores), 1, keepdims=True))
                probs = jnp.exp(scores - logsum)
                weights = probs.astype(bf16)
                got = mm(weights, vw).astype(bf16)
                delta = jnp.sum(gm.astype(f32) * got.astype(f32), 1, keepdims=True)
                prod = mm_cols(gm, vw)
                score_grad = (probs * (prod - delta) * scale).astype(bf16)
                mixed.append(got)
                dq.append(mm(score_grad, kw))
                dk[lo:hi, :] += mm_rows(score_grad, qm)
                dv[lo:hi, :] += mm_rows(weights, gm)
            act[at_q:hi, out_at] = jnp.where(lowb, mixed[0], mixed[1])
            dqs.append(jnp.where(lowb, dq[0], dq[1]))
        dquery = turn(jnp.concatenate(dqs, 0), -1.0)
        dkeys = swap(turn(dk[...], -1.0))
        dvals = dv[...]
        pg[:, pl.ds(at, LANES)] = jnp.where(lowq, dquery, dkeys).astype(bf16)
        pg[:, pl.ds(pl.multiple_of(at + LANES, LANES), LANES)] = jnp.where(
            lowq, dvals, dquery).astype(bf16)
        pg[:, pl.ds(pl.multiple_of(at + 2 * LANES, LANES), LANES)] = jnp.where(
            lowq, dkeys, dvals).astype(bf16)
        return carry

    lax.fori_loop(0, attn // LANES, pair_step, 0)

    landed(1)
    step = 2 * LANES

    def hidden_step(n, carry):
        at = pl.ds(pl.multiple_of(n * step, step), step)
        at_out = pl.ds(pl.multiple_of(attn + n * step, LANES), step)
        value = mm(si[...], wu[:, at])
        erf = 0.5 * (1.0 + lax.erf(value * inv_sqrt_two))
        act[:, at_out] = (value * erf).astype(bf16)
        slope = erf + value * inv_sqrt_two_pi * jnp.exp(-0.5 * value * value)
        hg[:, at] = (mm(co[...], wo[:, at_out]) * slope).astype(bf16)
        return carry

    lax.fori_loop(0, hidden // step, hidden_step, 0)

    def spread_rows(ref, at, value):
        value = value.astype(bf16)
        for r in range(row_count):
            ref[r, :LANES, at] = value[r * LANES:(r + 1) * LANES]
            ref[r, LANES:, at] = value[tail + r * small:tail + (r + 1) * small]

    def weight_grads(ref, left, right, size):
        count = size // step

        def one(n, carry):
            at = pl.ds(pl.multiple_of(n * step, step), step)
            spread_rows(ref, at, mm(left[...], right[:, at]))
            return carry

        lax.fori_loop(0, count, one, 0)
        if size % step:
            at = slice(count * step, size)
            spread_rows(ref, at, mm(left[...], right[:, at]))

    weight_grads(go, cot, act, act.shape[1])
    weight_grads(gu, sit, hg, hidden)
    weight_grads(gq, fit, pg, pg.shape[1])

    def put_tiles(ref, chunks):
        for r in range(row_count):
            ref[r, :length, :] = chunks[r].astype(bf16)
        for p in range(row_count // 2):
            both = chunks[row_count + p]
            top, bottom = both[:halflen], both[halflen:]
            ref[2 * p, length:, :] = jnp.where(low, top, swap(bottom)).astype(bf16)
            ref[2 * p + 1, length:, :] = jnp.where(low, swap(top), bottom).astype(bf16)

    def split(value):
        return [value[:, n * LANES:(n + 1) * LANES] for n in range(value.shape[1] // LANES)]

    out_tiles, back1, back2 = [], 0.0, 0.0
    sums = []
    for n in range(width // step):
        at = slice(n * step, (n + 1) * step)
        out_tiles += split(mm_cols(act[...], wo[at, :]))
        first = mm_cols(pg[...], wq[at, :])
        second = mm_cols(hg[...], wu[at, :])
        value = normed[:, at]
        gains = jnp.concatenate([norm_tile(2 * n), norm_tile(2 * n + 1)], 1)
        four = jnp.concatenate(
            [jnp.sum(first * value, 0, keepdims=True), jnp.sum(first, 0, keepdims=True),
             jnp.sum(second * value, 0, keepdims=True), jnp.sum(second, 0, keepdims=True),
             jnp.zeros((4, step), f32)], 0)
        sums += split(four)
        both = gains[0:1] * first + gains[2:3] * second
        comb[:, at] = both
        back1 = back1 + jnp.sum(both, 1, keepdims=True)
        back2 = back2 + jnp.sum(both * value, 1, keepdims=True)
    put_tiles(outp, out_tiles)
    grad_tiles = []
    for n in range(width // LANES):
        at = slice(n * LANES, (n + 1) * LANES)
        grad_tiles.append(
            rstd * (comb[:, at] - back1 / width - normed[:, at] * (back2 / width)))
    put_tiles(gradp, grad_tiles)
    for r in range(row_count):
        nrmp[r, :, :LANES] = sums[r]
    for p in range(row_count // 2):
        both = sums[row_count + p]
        nrmp[2 * p, :, LANES:] = both
        nrmp[2 * p + 1, :, LANES:] = swap(both)


def compute_all(row_count, width, segs, freq, xg, cg, ng, own, gathered):
    bf16, f32 = jnp.bfloat16, jnp.float32
    length = segs.shape[1]
    n = row_count
    vmem = pl.BlockSpec(memory_space=pltpu.VMEM)
    anywhere = pl.BlockSpec(memory_space=pl.ANY)
    sizes = [w.shape[1] for w in own]
    local = own[0].shape[0]
    return pl.pallas_call(
        functools.partial(compute_kernel, n, width),
        out_shape=[
            jax.ShapeDtypeStruct(xg.shape, bf16),
            jax.ShapeDtypeStruct(xg.shape, bf16),
            jax.ShapeDtypeStruct(ng.shape, f32),
        ] + [jax.ShapeDtypeStruct((n, local, s), bf16) for s in sizes],
        in_specs=[vmem] * 5 + [anywhere] * 6,
        out_specs=[vmem] * 6,
        scratch_shapes=[pltpu.VMEM((width, s), bf16) for s in sizes] + [
            pltpu.VMEM((length, width), f32),
            pltpu.VMEM((length, width), bf16),
            pltpu.VMEM((length, width), bf16),
            pltpu.VMEM((length, width), bf16),
            pltpu.VMEM((width, length), bf16),
            pltpu.VMEM((width, length), bf16),
            pltpu.VMEM((width, length), bf16),
            pltpu.VMEM((length, sizes[0] // 3), bf16),
            pltpu.VMEM((length, sizes[2]), bf16),
            pltpu.VMEM((length, sizes[1]), bf16),
            pltpu.VMEM((length, sizes[0]), bf16),
            pltpu.VMEM((length, width), f32),
            pltpu.VMEM((length, LANES), f32),
            pltpu.VMEM((length, LANES), f32),
            pltpu.SemaphoreType.DMA((2, 3, n)),
        ],
        compiler_params=pltpu.CompilerParams(vmem_limit_bytes=56 << 20),
        name="compute",
    )(segs, freq, xg, cg, ng, *own, *gathered)


def pack_tokens(rows, length):
    blocks = rows.reshape(-1, length, rows.shape[1])
    ends = blocks[:, :, LANES:]
    joined = jnp.concatenate([ends[:, :length // 2], ends[:, length // 2:]], 2)
    return jnp.concatenate([blocks[:, :, :LANES], joined], 1)


def unpack_tokens(blocks, length):
    joined = blocks[:, length:]
    small = joined.shape[2] // 2
    ends = jnp.concatenate([joined[:, :, :small], joined[:, :, small:]], 1)
    return jnp.concatenate([blocks[:, :length], ends], 2).reshape(-1, LANES + small)


def on_device(
    tokens_in,
    out_cot,
    segments,
    norm_params,
    qkv_weight,
    proj_weight,
    up_weight,
    down_weight,
    norm_first,
    norm_second,
    qkv_first,
    qkv_second,
    proj_first,
    proj_second,
    up_first,
    up_second,
    down_first,
    down_second,
):
    row_count = lax.axis_size("row")
    data_count = lax.axis_size("dp")
    col_count = lax.axis_size("col")
    local_count, local_width = tokens_in.shape
    width = local_width * row_count
    length = segments.shape[1]
    shares = local_count // length
    bf16 = jnp.bfloat16

    proj_t, down_t = proj_weight.T, down_weight.T
    own = (
        qkv_weight.astype(bf16),
        up_weight.astype(bf16),
        jnp.concatenate([proj_t.astype(bf16), down_t.astype(bf16)], 1),
    )
    nrm = jnp.pad(norm_params, ((0, 4), (0, 2 * LANES - local_width)))
    xg, cg, ng, *gathered = gather_all(
        row_count, pack_tokens(tokens_in, length), pack_tokens(out_cot, length), nrm, own)

    half = ROT_DIM // 2
    freq = rotary_base ** (-2.0 * jnp.arange(half, dtype=jnp.float32) / ROT_DIM)
    freq = jnp.concatenate([freq, freq, jnp.zeros(HEAD_DIM - ROT_DIM, jnp.float32)])
    freq = jnp.broadcast_to(jnp.tile(freq, 2)[None], (8, LANES))
    outp, gradp, nrmp, *parts = compute_all(
        row_count, width, segments, freq, xg, cg, ng, own, gathered)
    out_sum, grad_sum, norm_sum, qkv_sum, up_sum, out_w = reduce_all(
        row_count, data_count, shares, outp, gradp, nrmp, parts)

    output = (tokens_in.astype(jnp.float32)
              + unpack_tokens(out_sum, length).astype(jnp.float32)).astype(bf16)
    input_grad = (out_cot.astype(jnp.float32)
                  + unpack_tokens(grad_sum, length).astype(jnp.float32)).astype(bf16)
    norm_grad = norm_sum[:4, :local_width]
    qkv_grad = qkv_sum.astype(jnp.float32)
    up_grad = up_sum.astype(jnp.float32)
    attn_width = proj_weight.shape[0]
    proj_grad = out_w[:, :attn_width].astype(jnp.float32).T
    down_grad = out_w[:, attn_width:].astype(jnp.float32).T
    norm_new, norm_first_new, norm_second_new = adam_update(
        norm_params, norm_first, norm_second, norm_grad, 0.0
    )
    qkv_new, qkv_first_new, qkv_second_new = adam_update(
        qkv_weight, qkv_first, qkv_second, qkv_grad, decay_rate
    )
    proj_new, proj_first_new, proj_second_new = adam_update(
        proj_weight, proj_first, proj_second, proj_grad, decay_rate
    )
    up_new, up_first_new, up_second_new = adam_update(
        up_weight, up_first, up_second, up_grad, decay_rate
    )
    down_new, down_first_new, down_second_new = adam_update(
        down_weight, down_first, down_second, down_grad, decay_rate
    )
    return (
        output,
        input_grad,
        norm_grad,
        qkv_grad,
        proj_grad,
        up_grad,
        down_grad,
        norm_new,
        qkv_new,
        proj_new,
        up_new,
        down_new,
        norm_first_new,
        norm_second_new,
        qkv_first_new,
        qkv_second_new,
        proj_first_new,
        proj_second_new,
        up_first_new,
        up_second_new,
        down_first_new,
        down_second_new,
    )


def solution(mesh):
    placed = (
        P(("dp", "col"), "row"),
        P(("dp", "col"), "row"),
        P("dp", None),
        P(None, "row"),
        P("row", "col"),
        P("col", "row"),
        P("row", "col"),
        P("col", "row"),
        P(None, "row"),
        P(None, "row"),
        P("row", "col"),
        P("row", "col"),
        P("col", "row"),
        P("col", "row"),
        P("row", "col"),
        P("row", "col"),
        P("col", "row"),
        P("col", "row"),
    )
    return jax.shard_map(
        on_device,
        mesh=mesh,
        in_specs=placed,
        out_specs=(
            P(("dp", "col"), "row"),
            P(("dp", "col"), "row"),
            P(None, "row"),
            P("row", "col"),
            P("col", "row"),
            P("row", "col"),
            P("col", "row"),
            P(None, "row"),
            P("row", "col"),
            P("col", "row"),
            P("row", "col"),
            P("col", "row"),
            P(None, "row"),
            P(None, "row"),
            P("row", "col"),
            P("row", "col"),
            P("col", "row"),
            P("col", "row"),
            P("row", "col"),
            P("row", "col"),
            P("col", "row"),
            P("col", "row"),
        ),
        check_vma=False,
    )
```

time: 317 us -> 224 us (0.71)
  Pallas kernels: 0 us -> 177 us
  blocking collectives: 141 us -> 0 us
  matrix products: 47.2 us -> 0 us
  waiting for transfers between devices: 21.7 us -> 0 us
  starting transfers between devices: 21 us -> 0 us
  local copies, waits for them, and re-layouts: 42.1 us -> 24.6 us
  between operations: 15.2 us -> 0.96 us
  other arithmetic: 25.5 us -> 19.2 us
    pallas_call x0 -> x3, Pallas kernels: none -> 177 us  [the longest x1 72.3 us: reduce_all(): pl.pallas_call(functools.partial(reduce_kernel, row_count, groups_out), o...]
    all_gather x6 -> x0, blocking collectives: 83.4 us -> none  [the longest x1 40.2 us: on_device(): norm_full = lax.all_gather(norm_params, 'row', axis=1, tiled=True)]
    psum x1 -> x0, blocking collectives: 57.2 us -> none  [on_device(): lax.psum(norm_part, ('dp', 'row', 'col'))]
    dot_general x14 -> x0, matrix products: 39.8 us -> none  [the longest x3 12.5 us: dot32(): return jnp.dot(left, right, preferred_element_type=jnp.float32)]
    all_to_all x4 -> x0, starting transfers between devices: 16.6 us -> none  [the longest x2 9.31 us: to_tokens(): blocks = lax.all_to_all(blocks, 'row', 0, 0, tiled=True)]
    all_to_all x4 -> x0, waiting for transfers between devices: 15.9 us -> none  [the longest x2 11.4 us: to_features(): blocks = lax.all_to_all(jnp.moveaxis(blocks, 1, 0), 'row', 0, 0, tiled=True)]
    reduce_sum x1 -> x0, matrix products: 7.4 us -> none  [attend(): total = jnp.sum(jnp.exp(scores), -1, keepdims=True)]
    ppermute x2 -> x0, waiting for transfers between devices: 5.8 us -> none  [to_features(): total = total + lax.ppermute(sent, 'col', ring).astype(jnp.float32)]
  transfers between devices with their start and end apart: 8 -> 0, of which waited for: 3 -> 0; matrix products, arithmetic and copies ran while one was open for 12% -> 0% of each run, Pallas kernels for 0% -> 0%
where the time goes in v1:
time: 224 us; the launch traced here: 222 us
  Pallas kernels  177 us (79%)
  local copies, waits for them, and re-layouts  24.6 us (11%)
  other arithmetic  19.2 us (9%)
    pallas_call x1, Pallas kernels, reduce_all(): pl.pallas_call(functools.partial(reduce_kernel, row_count, groups_out), o...  72.3 us
    pallas_call x1, Pallas kernels, gather_all(): pl.pallas_call(functools.partial(gather_kernel, row_count), out_shape=[ja...  65.2 us
    pallas_call x1, Pallas kernels, compute_all(): pl.pallas_call(functools.partial(compute_kernel, n, width), out_shape=[ja...  39.7 us
    unnamed x66, local copies, waits for them, and re-layouts  17.9 us
    sub x5, other arithmetic, adam_update(): weight - learn_rate * (first_hat / (jnp.sqrt(second_hat) + adam_eps) + de...  10.1 us

profile of v1, /device:TPU:0, one launch (start us, length us, event | category | flops | bytes accessed | tf_op | source)
XLA Modules:
  0.0 221.9 jit_solution(13603856380590324737)
XLA Ops:
  2.2 1.0 convert_bitcast_fusion.3
  3.1 1.2 convert_element_type.53.w0
  6.0 1.0 copy-done.15
  8.3 65.2 %gather.1 = (bf16[4,768,128]{2,1,0:T(8,128)(2,1)S(1)}, bf16[4,768,128]{2,1,0:T(8,128)(2,1)S(1)}, f32[4,8,256]{2,1,0:T(8,128)S(1)}, bf16[4,192,1152]{2,1,0:T(8,12...) custom-call(bf16[2,768,128]{2,1,0:T(8,128)(2,1)S(1)} %get-tuple-element.86.tok, ...), custom_call_target="tpu_custom_call" | custom-call | bytes 3342336 | tf_op jit(solution)/shard_map/gather/pallas_call | solution.py:309
  73.5 1.6 copy-done.3
  75.0 1.5 copy-done.5
  76.5 1.3 copy-done.7
  78.7 0.9 copy-done.11
  80.1 39.7 %compute.1 = (bf16[4,768,128]{2,1,0:T(8,128)(2,1)}, bf16[4,768,128]{2,1,0:T(8,128)(2,1)}, f32[4,8,256]{2,1,0:T(8,128)}, bf16[4,192,1152]{2,1,0:T(8,128)(2,1)}, b...) custom-call(s32[4,512]{1,0:T(4,128)} %seg_ref.1, f32[8,128]{1,0:T(8,128)} %broadcast_in_dim.12.freq_ref, ...), custom_call_target="tpu_custom_call" | custom-call | tf_op jit(solution)/shard_map/compute/pallas_call | solution.py:940
  119.9 1.7 copy-done.4
  121.6 1.5 copy-done.6
  123.0 1.1 copy-done.8
  124.2 1.1 copy-done.9
  126.1 72.3 %reduce.1 = (bf16[2,768,128]{2,1,0:T(8,128)(2,1)S(1)}, bf16[2,768,128]{2,1,0:T(8,128)(2,1)S(1)}, f32[8,256]{1,0:T(8,128)S(1)}, bf16[192,1152]{1,0:T(8,128)(2,1)S...) custom-call(bf16[4,768,128]{2,1,0:T(8,128)(2,1)S(1)} %copy-done.8, bf16[4,768,128]{2,1,0:T(8,128)(2,1)S(1)} %copy-done.9, ...), custom_call_target="tpu_custom_call" | custom-call | bytes 16777216 | tf_op jit(solution)/shard_map/reduce/pallas_call | solution.py:633
  199.5 1.1 bitcast_convert_fusion
  200.6 2.4 %copy.43 = f32[1024,192]{0,1:T(8,128)} copy(f32[1024,192]{1,0:T(8,128)} %bitcast_convert_fusion) | data formatting | bytes 1572864 | tf_op jit(solution)/shard_map/convert_element_type | solution.py:1036
  203.0 2.1 add_convert_fusion
  205.1 1.1 bitcast_convert_fusion.1
  206.2 2.5 %copy.42 = f32[1024,192]{0,1:T(8,128)} copy(f32[1024,192]{1,0:T(8,128)} %bitcast_convert_fusion.1) | data formatting | bytes 1572864 | tf_op jit(solution)/shard_map/convert_element_type | solution.py:1034
  208.6 2.1 add_convert_fusion.1
  210.7 2.2 multiply_subtract_fusion.3
  212.9 2.0 multiply_subtract_fusion.2
  215.8 2.8 %multiply_subtract_fusion = (f32[1536,192]{0,1:T(8,128)}, f32[1536,192]{0,1:T(8,128)}, f32[1536,192]{0,1:T(8,128)}, f32[1536,192]{0,1:T(8,128)}) fusion(f32[1536,192]{0,1:T(8,128)S(1)} %copy-done.14, f32[1536,192]{0,1:T(8,128)S(1)} %copy-done.21, f32[1536,192]{0,1:T(8,128)S(1)} %copy-done.22, bf16[192,1920]{1,0:T(8,128)(2,1)S(1)} %get-tuple-element.56), kind=kLoop, calls=%fused_computation.6 | loop fusion | flops 4718592 | bytes 8847360 | tf_op jit(solution)/shard_map/sub | solution.py:35
  219.4 2.6 %multiply_subtract_fusion.1 = (f32[192,1536]{1,0:T(8,128)}, f32[192,1536]{1,0:T(8,128)}, f32[192,1536]{1,0:T(8,128)}, f32[192,1536]{1,0:T(8,128)}) fusion(f32[192,1536]{1,0:T(8,128)S(1)} %copy-done.16, f32[192,1536]{1,0:T(8,128)S(1)} %copy-done.23, f32[192,1536]{1,0:T(8,128)S(1)} %copy-done.24, bf16[192,1536]{1,0:T(8,128)(2,1)S(1)} %get-tuple-element.57), kind=kLoop, calls=%fused_computation.8 | loop fusion | flops 4718592 | bytes 8847360 | tf_op jit(solution)/shard_map/sub | solution.py:35
  (79 shorter events, 9.4 us)
Async XLA Ops:
  0.7 3.7 %copy-start.19 = (bf16[1024,192]{0,1:T(8,128)(2,1)S(1)}, bf16[1024,192]{0,1:T(8,128)(2,1)}, u32[]{:S(2)}) copy-start(bf16[1024,192]{0,1:T(8,128)(2,1)} %param.18) | copy-start | bytes 1179652
  4.4 3.2 %copy-start.2 = (bf16[192,1152]{1,0:T(8,128)(2,1)}, bf16[192,1152]{1,0:T(8,128)(2,1)S(1)}, u32[]{:S(2)}) copy-start(bf16[192,1152]{1,0:T(8,128)(2,1)S(1)} %convert_element_type.53.w0) | copy-start | bytes 1327108
  5.8 1.3 copy-start.15
  6.0 1.4 copy-start.14
  8.3 65.2 %copy-start = (bf16[192,1920]{1,0:T(8,128)(2,1)}, bf16[192,1920]{1,0:T(8,128)(2,1)S(1)}, u32[]{:S(2)}) copy-start(bf16[192,1920]{1,0:T(8,128)(2,1)S(1)} %pad_maximum_fusion.w2) | copy-start | bytes 2211844
  73.5 1.6 copy-start.3
  75.0 1.5 copy-start.5
  76.5 1.3 copy-start.7
  119.9 1.7 copy-start.4
  121.6 1.5 copy-start.6
  126.1 72.3 %copy-start.29 = (f32[4,192]{1,0:T(4,128)S(1)}, f32[4,192]{1,0:T(4,128)}, u32[]{:S(2)}) copy-start(f32[4,192]{1,0:T(4,128)} %param.21) | copy-start | bytes 9220
  126.1 72.3 %copy-start.30 = (f32[4,192]{1,0:T(4,128)S(1)}, f32[4,192]{1,0:T(4,128)}, u32[]{:S(2)}) copy-start(f32[4,192]{1,0:T(4,128)} %param.26) | copy-start | bytes 9220
  126.1 72.3 %copy-start.31 = (f32[4,192]{1,0:T(4,128)S(1)}, f32[4,192]{1,0:T(4,128)}, u32[]{:S(2)}) copy-start(f32[4,192]{1,0:T(4,128)} %param.27) | copy-start | bytes 9220
  206.2 2.5 %copy-start.20 = (bf16[1024,192]{0,1:T(8,128)(2,1)S(1)}, bf16[1024,192]{0,1:T(8,128)(2,1)}, u32[]{:S(2)}) copy-start(bf16[1024,192]{0,1:T(8,128)(2,1)} %param.18) | copy-start | bytes 1179652
  208.6 2.1 copy-start.25
  208.6 2.1 copy-start.28
  208.6 4.3 %copy-start.27 = (f32[192,1152]{1,0:T(8,128)S(1)}, f32[192,1152]{1,0:T(8,128)}, u32[]{:S(2)}) copy-start(f32[192,1152]{1,0:T(8,128)} %param.29) | copy-start | bytes 2654212
  210.7 2.2 copy-start.17
  210.7 2.2 copy-start.26
  212.9 2.0 copy-start.21
  212.9 2.8 %copy-start.22 = (f32[1536,192]{0,1:T(8,128)S(1)}, f32[1536,192]{0,1:T(8,128)}, u32[]{:S(2)}) copy-start(f32[1536,192]{0,1:T(8,128)} %param.35) | copy-start | bytes 3538948
  215.8 2.8 %copy-start.16 = (f32[192,1536]{1,0:T(8,128)S(1)}, f32[192,1536]{1,0:T(8,128)}, u32[]{:S(2)}) copy-start(f32[192,1536]{1,0:T(8,128)} %param.24) | copy-start | bytes 3538948
  215.8 2.8 %copy-start.23 = (f32[192,1536]{1,0:T(8,128)S(1)}, f32[192,1536]{1,0:T(8,128)}, u32[]{:S(2)}) copy-start(f32[192,1536]{1,0:T(8,128)} %param.32) | copy-start | bytes 3538948
  215.8 3.6 %copy-start.24 = (f32[192,1536]{1,0:T(8,128)S(1)}, f32[192,1536]{1,0:T(8,128)}, u32[]{:S(2)}) copy-start(f32[192,1536]{1,0:T(8,128)} %param.33) | copy-start | bytes 3538948
  (8 other events, 7.4 us)

commit v2 on v0

v2 whole, which is shorter than its diff:
```python
import functools
import math
import types

import jax
import jax.numpy as jnp
from jax import lax
from jax.experimental import pallas as pl
from jax.experimental.pallas import tpu as pltpu
from jax.sharding import PartitionSpec as P

D = 768
HEAD_DIM = 64
ROT_DIM = 16
SEQ_LEN = 512
STEP = 3


norm_eps = 1e-05
rotary_base = 10000.0
learn_rate = 0.01
beta_first = 0.9
beta_second = 0.95
adam_eps = 1e-08
decay_rate = 0.1
mask_fill = -1e30
inv_sqrt_two = 0.7071067811865476
inv_sqrt_two_pi = 0.3989422804014327


def adam_update(weight, first, second, grad, decay):
    first_new = beta_first * first + (1.0 - beta_first) * grad
    second_new = beta_second * second + (1.0 - beta_second) * grad * grad
    first_hat = first_new / (1.0 - beta_first**STEP)
    second_hat = second_new / (1.0 - beta_second**STEP)
    weight_new = weight - learn_rate * (
        first_hat / (jnp.sqrt(second_hat) + adam_eps) + decay * weight
    )
    return (weight_new, first_new, second_new)


MESH = pl.DeviceIdType.MESH
LANES = 128
QUARTERS = 4
WINDOW = 256
QBLOCK = 128


def remote(src, dst, send_sem, recv_sem, device):
    return pltpu.make_async_remote_copy(
        src_ref=src,
        dst_ref=dst,
        send_sem=send_sem,
        recv_sem=recv_sem,
        device_id=device,
        device_id_type=MESH,
    )


def places(row_count):
    data, row, col = lax.axis_index("dp"), lax.axis_index("row"), lax.axis_index("col")
    quarter = lax.rem(data, QUARTERS)
    far = data - quarter + lax.rem(quarter + 2, QUARTERS)
    mate = data + 1 - 2 * lax.rem(quarter, 2)
    return data, row, col, quarter, far, mate


def greet(peers):
    barrier = pltpu.get_barrier_semaphore()
    for peer in peers:
        pl.semaphore_signal(barrier, inc=1, device_id=peer, device_id_type=MESH)
    pl.semaphore_wait(barrier, len(peers))


def gatherer(row_count, at, tok, cot, nrm, own_w, all_w, s):
    data, row, col, quarter, far, mate = at
    shares = tok.shape[0]
    other = 1 - col
    home = lax.div(row, shares)
    groups = len(own_w)
    local = own_w[0].shape[0]
    depth = local // QUARTERS
    others = [lax.rem(row + k, row_count) for k in range(1, row_count)]

    def rows(src, part):
        return pl.ds(pl.multiple_of(src * local + part * depth, depth), depth)

    def step_copy(g, src, up):
        ref = all_w[g].at[rows(src, quarter)]
        return remote(ref, ref, s.z_s.at[int(up), g, src], s.z_r.at[g, src],
                      (data, row + 1 if up else row - 1, col))

    def own_copy(g, up):
        return remote(own_w[g].at[rows(0, quarter)], all_w[g].at[rows(row, quarter)],
                      s.z_s.at[int(up), g, row], s.z_r.at[g, row],
                      (data, row + 1 if up else row - 1, col))

    def own_local(g):
        dest = all_w[g].at[pl.ds(pl.multiple_of(row * local, local), local)]
        return pltpu.make_async_copy(own_w[g], dest, s.own_l.at[g])

    def far_copy(g, src):
        ref = all_w[g].at[rows(src, quarter)]
        return remote(ref, ref, s.f_s.at[g, src], s.f_r.at[g, src], (far, row, col))

    def far_wait(g, src):
        ref = all_w[g].at[rows(src, lax.rem(quarter + 2, QUARTERS))]
        remote(ref, ref, s.f_s.at[g, src], s.f_r.at[g, src], (far, row, col)).wait_recv()

    def mate_copy(g, src, second):
        part = lax.rem(quarter + 2, QUARTERS) if second else quarter
        ref = all_w[g].at[rows(src, part)]
        return remote(ref, ref, s.m_s.at[int(second), g, src], s.m_r.at[int(second), g, src],
                      (mate, row, col))

    def mate_wait(g, src, second):
        theirs = quarter + 1 - 2 * lax.rem(quarter, 2)
        part = lax.rem(theirs + 2, QUARTERS) if second else theirs
        ref = all_w[g].at[rows(src, part)]
        remote(ref, ref, s.m_s.at[int(second), g, src], s.m_r.at[int(second), g, src],
               (mate, row, col)).wait_recv()

    def norm_copy(k):
        return remote(nrm, s.ng.at[row], s.nrm_s.at[k], s.nrm_r.at[row], (data, others[k], col))

    def norm_wait(k):
        remote(nrm, s.ng.at[others[k]], s.nrm_s.at[k], s.nrm_r.at[others[k]],
               (data, others[k], col)).wait_recv()

    def norm_local():
        return pltpu.make_async_copy(nrm, s.ng.at[row], s.loc.at[2])

    def token_copy(j):
        return remote(tok.at[j], s.xg.at[row], s.x_s.at[j], s.x_r.at[row],
                      (data, col * shares + j, col))

    def token_local(j):
        return pltpu.make_async_copy(tok.at[j], s.xg.at[row], s.loc.at[0])

    def hop_copy(j):
        return remote(cot.at[j], s.hop.at[j], s.h_s.at[j], s.h_r.at[j], (data, row, other))

    def cot_copy(j):
        return remote(s.hop.at[j], s.cg.at[row], s.c_s.at[j], s.c_r.at[row],
                      (data, other * shares + j, col))

    def cot_local(j):
        return pltpu.make_async_copy(s.hop.at[j], s.cg.at[row], s.loc.at[1])

    def x_wait(src):
        remote(tok.at[0], s.xg.at[src], s.x_s.at[0], s.x_r.at[src],
               (data, src, col)).wait_recv()

    def c_wait(src):
        remote(tok.at[0], s.cg.at[src], s.c_s.at[0], s.c_r.at[src],
               (data, src, col)).wait_recv()

    def across(which, src):
        ref, send, recv = ((s.xg, s.xy_s, s.xy_r), (s.cg, s.cy_s, s.cy_r))[which]
        return remote(ref.at[src], ref.at[src], send.at[src], recv.at[src],
                      (data, row, other))

    mains = (col == home, col != home)

    def begin():
        for k in range(row_count - 1):
            norm_copy(k).start()
        norm_local().start()
        for j in range(shares):
            @pl.when(col * shares + j != row)
            def _():
                token_copy(j).start()

            @pl.when(col * shares + j == row)
            def _():
                token_local(j).start()
            hop_copy(j).start()
        for g in range(groups):
            own_local(g).start()

    def send_own(g):
        @pl.when(row + 1 < row_count)
        def _():
            own_copy(g, True).start()

        @pl.when(row > 0)
        def _():
            own_copy(g, False).start()

    def cot_hop():
        for j in range(shares):
            hop_copy(j).wait_recv()

            @pl.when(other * shares + j != row)
            def _():
                cot_copy(j).start()

            @pl.when(other * shares + j == row)
            def _():
                cot_local(j).start()

    def forward(which):
        @pl.when(mains[which])
        def _():
            (token_local, cot_local)[which](0).wait()
            across(which, row).start()
            for src in others:
                (x_wait, c_wait)[which](src)
                across(which, src).start()

    def arrived(which):
        @pl.when(jnp.logical_not(mains[which]))
        def _():
            for src in range(row_count):
                across(which, src).wait_recv()

    def norm_arrived():
        norm_local().wait()
        for k in range(row_count - 1):
            norm_wait(k)

    pending = []

    def settle():
        for g, k, below in pending:
            src = row - k if below else row + k

            @pl.when(src >= 0 if below else src < row_count)
            def _():
                far_wait(g, src)
                mate_copy(g, src, True).start()
        pending.clear()

    def relay(g, k):
        now = []
        for below in (True, False):
            src = row - k if below else row + k

            @pl.when(src >= 0 if below else src < row_count)
            def _():
                step_copy(g, src, below).wait_recv()
                onward = row + 1 < row_count if below else row > 0

                @pl.when(onward)
                def _():
                    step_copy(g, src, below).start()
                far_copy(g, src).start()
                mate_copy(g, src, False).start()
            now.append((g, k, below))
        settle()
        pending.extend(now)

    def landed(g):
        own_local(g).wait()
        for k in range(1, row_count):
            for second in (False, True):
                mate_wait(g, others[k - 1], second)

    def drain():
        for which in range(2):
            @pl.when(mains[which])
            def _():
                for src in range(row_count):
                    across(which, src).wait_send()
        for k in range(row_count - 1):
            norm_copy(k).wait_send()
        for j in range(shares):
            @pl.when(col * shares + j != row)
            def _():
                token_copy(j).wait_send()

            @pl.when(other * shares + j != row)
            def _():
                cot_copy(j).wait_send()
            hop_copy(j).wait_send()
        for g in range(groups):
            @pl.when(row + 1 < row_count)
            def _():
                own_copy(g, True).wait_send()

            @pl.when(row > 0)
            def _():
                own_copy(g, False).wait_send()
            for k in range(1, row_count):
                for below in (True, False):
                    src = row - k if below else row + k

                    @pl.when(src >= 0 if below else src < row_count)
                    def _():
                        onward = row + 1 < row_count if below else row > 0

                        @pl.when(onward)
                        def _():
                            step_copy(g, src, below).wait_send()
                        far_copy(g, src).wait_send()
                        for second in (False, True):
                            mate_copy(g, src, second).wait_send()

    return types.SimpleNamespace(
        begin=begin, send_own=send_own, cot_hop=cot_hop, forward=forward, arrived=arrived,
        norm_arrived=norm_arrived, settle=settle, relay=relay, landed=landed, drain=drain)


def reducer(row_count, groups_out, at, parts, total, out_t, grad_t, nrm_t, s):
    data, row, col, quarter, far, mate = at
    groups = len(parts)
    shares = out_t.shape[0]
    other = 1 - col
    home = lax.div(row, shares)
    local = parts[0].shape[0] // row_count
    depth = local // QUARTERS
    data_count = QUARTERS * groups_out
    block = lax.div(data, QUARTERS)
    others = [lax.rem(row + k, row_count) for k in range(1, row_count)]
    order = others + [row]
    wider = [lax.rem(data + QUARTERS * k, data_count) for k in range(1, groups_out)]
    everyone = [lax.rem(data + k, data_count) for k in range(1, data_count)]
    f32, bf16 = jnp.float32, jnp.bfloat16
    half = lax.rem(quarter + 2, QUARTERS)
    theirs = quarter + 1 - 2 * lax.rem(quarter, 2)
    theirs_half = lax.rem(theirs + 2, QUARTERS)
    slot = row - home * shares

    def rows(t, part):
        return pl.ds(pl.multiple_of(t * local + part * depth, depth), depth)

    def norm_z(k):
        return remote(s.nrmp.at[others[k]], s.nz.at[row], s.nz_s.at[k], s.nz_r.at[row],
                      (data, others[k], col))

    def norm_z_wait(k):
        remote(s.nrmp.at[0], s.nz.at[others[k]], s.nz_s.at[k], s.nz_r.at[others[k]],
               (data, others[k], col)).wait_recv()

    def norm_c():
        return remote(s.nrm1, s.nc, s.nc_s.at[0], s.nc_r.at[0], (data, row, other))

    def norm_d(k):
        return remote(s.nrm2, s.nd.at[data], s.nd_s.at[k], s.nd_r.at[data],
                      (everyone[k], row, col))

    def norm_d_wait(k):
        remote(s.nrm2, s.nd.at[everyone[k]], s.nd_s.at[k], s.nd_r.at[everyone[k]],
               (everyone[k], row, col)).wait_recv()

    def out_y(t):
        return remote(s.outp.at[t], s.oy.at[t], s.oy_s.at[t], s.oy_r.at[t], (data, row, other))

    def grad_y(t):
        return remote(s.gradp.at[t], s.gy.at[t], s.gy_s.at[t], s.gy_r.at[t],
                      (data, row, other))

    def out_z(t):
        return remote(s.od.at[t], out_t.at[slot], s.oz_s.at[t], s.oz_r.at[slot],
                      (data, t, col))

    def out_local():
        return pltpu.make_async_copy(s.od.at[row], out_t.at[slot], s.loc.at[3])

    def out_z_wait(j):
        remote(s.od.at[0], out_t.at[j], s.oz_s.at[0], s.oz_r.at[j],
               (data, row, col)).wait_recv()

    def grad_z(t):
        return remote(s.gd.at[t], s.gh.at[slot], s.gz_s.at[t], s.gz_r.at[slot],
                      (data, t, col))

    def grad_local():
        return pltpu.make_async_copy(s.gd.at[row], s.gh.at[slot], s.loc.at[4])

    def grad_z_wait(j):
        remote(s.gd.at[0], s.gh.at[j], s.gz_s.at[0], s.gz_r.at[j],
               (data, row, col)).wait_recv()

    def grad_h(j):
        return remote(s.gh.at[j], grad_t.at[j], s.gh_s.at[j], s.gh_r.at[j], (data, row, other))

    def mate_part(g, t, second):
        part = theirs_half if second else theirs
        return remote(parts[g].at[rows(t, part)], s.crecv[g].at[int(second), t],
                      s.pc_s.at[int(second), g, t], s.pc_r.at[int(second), g, t],
                      (mate, row, col))

    def far_part(g, t):
        return remote(s.fsend[g].at[t], s.frecv[g].at[t], s.pf_s.at[g, t], s.pf_r.at[g, t],
                      (far, row, col))

    def row_part(g, t):
        return remote(s.zsend[g].at[t], s.zrecv[g].at[row], s.pz_s.at[g, t], s.pz_r.at[g, row],
                      (data, t, col))

    def row_wait(g, src):
        remote(s.zsend[g].at[src], s.zrecv[g].at[src], s.pz_s.at[g, src], s.pz_r.at[g, src],
               (data, src, col)).wait_recv()

    def wide_part(g, k):
        return remote(total[g].at[rows(0, quarter)], s.extra[g].at[block],
                      s.e_s.at[g, k], s.e_r.at[g, block], (wider[k], row, col))

    def wide_wait(g, k):
        src = lax.div(wider[k], QUARTERS)
        remote(total[g].at[rows(0, quarter)], s.extra[g].at[src],
               s.e_s.at[g, k], s.e_r.at[g, src], (wider[k], row, col)).wait_recv()

    def far_sum(g):
        ref = total[g].at[rows(0, quarter)]
        return remote(ref, ref, s.a_s.at[g], s.a_r.at[g], (far, row, col))

    def far_sum_wait(g):
        ref = total[g].at[rows(0, half)]
        remote(ref, ref, s.a_s.at[g], s.a_r.at[g], (far, row, col)).wait_recv()

    def mate_sum(g, second):
        ref = total[g].at[rows(0, half if second else quarter)]
        return remote(ref, ref, s.b_s.at[int(second), g], s.b_r.at[int(second), g],
                      (mate, row, col))

    def mate_sum_wait(g, second):
        ref = total[g].at[rows(0, theirs_half if second else theirs)]
        remote(ref, ref, s.b_s.at[int(second), g], s.b_r.at[int(second), g],
               (mate, row, col)).wait_recv()

    o_main = col == home
    g_main = col != home

    def start(g):
        for t in order:
            mate_part(g, t, True).start()
        for t in order:
            mate_part(g, t, False).start()

    def start_out():
        @pl.when(jnp.logical_not(o_main))
        def _():
            for t in order:
                out_y(t).start()

    def start_grad():
        @pl.when(jnp.logical_not(g_main))
        def _():
            for t in order:
                grad_y(t).start()

    def start_norm():
        for k in range(row_count - 1):
            norm_z(k).start()

    def stage_far(g, t):
        mate_part(g, t, True).wait_recv()
        own = parts[g][rows(t, half), :].astype(f32)
        s.fsend[g][t] = (own + s.crecv[g][1, t].astype(f32)).astype(bf16)
        far_part(g, t).start()

    def stage_row(g, t):
        mate_part(g, t, False).wait_recv()
        far_part(g, t).wait_recv()
        mine = parts[g][rows(t, quarter), :].astype(f32)
        mine = mine + s.crecv[g][0, t].astype(f32) + s.frecv[g][t].astype(f32)
        s.zsend[g][t] = mine.astype(bf16)
        if t is not row:
            row_part(g, t).start()

    def outputs_out():
        @pl.when(o_main)
        def _():
            for t in order:
                out_y(t).wait_recv()
                s.od[t] = (s.outp[t].astype(f32) + s.oy[t].astype(f32)).astype(bf16)
                if t is row:
                    out_local().start()
                else:
                    out_z(t).start()

    def outputs_grad():
        @pl.when(g_main)
        def _():
            for t in order:
                grad_y(t).wait_recv()
                s.gd[t] = (s.gradp[t].astype(f32) + s.gy[t].astype(f32)).astype(bf16)
                if t is row:
                    grad_local().start()
                else:
                    grad_z(t).start()

    def grads_home():
        for j in range(shares):
            @pl.when(other * shares + j != row)
            def _():
                grad_z_wait(j)

            @pl.when(other * shares + j == row)
            def _():
                grad_local().wait()
            grad_h(j).start()

    def norm_rows():
        acc = s.nrmp[row]
        for k in range(row_count - 1):
            norm_z_wait(k)
            acc = acc + s.nz[others[k]]
        s.nrm1[...] = acc
        norm_c().start()

    def norm_cols():
        norm_c().wait_recv()
        s.nrm2[...] = s.nrm1[...] + s.nc[...]
        for k in range(len(everyone)):
            norm_d(k).start()

    def norm_last():
        acc = s.nrm2[...]
        for k in range(len(everyone)):
            norm_d_wait(k)
            acc = acc + s.nd[everyone[k]]
        nrm_t[...] = acc

    def finish(g):
        acc = s.zsend[g][row].astype(f32)
        for src in others:
            row_wait(g, src)
            acc = acc + s.zrecv[g][src].astype(f32)
        total[g][rows(0, quarter), :] = acc.astype(bf16)
        if wider:
            for k in range(len(wider)):
                wide_part(g, k).start()
            for k in range(len(wider)):
                wide_wait(g, k)
                acc = acc + s.extra[g][lax.div(wider[k], QUARTERS)].astype(f32)
            for k in range(len(wider)):
                wide_part(g, k).wait_send()
            total[g][rows(0, quarter), :] = acc.astype(bf16)
        far_sum(g).start()
        mate_sum(g, False).start()

    def spread(g):
        far_sum_wait(g)
        mate_sum(g, True).start()

    def drain():
        @pl.when(jnp.logical_not(o_main))
        def _():
            for t in range(row_count):
                out_y(t).wait_send()

        @pl.when(jnp.logical_not(g_main))
        def _():
            for t in range(row_count):
                grad_y(t).wait_send()

        @pl.when(o_main)
        def _():
            out_local().wait()
            for t in others:
                out_z(t).wait_send()

        @pl.when(g_main)
        def _():
            for t in others:
                grad_z(t).wait_send()
        for j in range(shares):
            @pl.when(col * shares + j != row)
            def _():
                out_z_wait(j)
            grad_h(j).wait()
        for k in range(row_count - 1):
            norm_z(k).wait_send()
        norm_c().wait_send()
        for k in range(len(everyone)):
            norm_d(k).wait_send()
        for g in range(groups):
            for t in range(row_count):
                for second in (False, True):
                    mate_part(g, t, second).wait_send()
                far_part(g, t).wait_send()
            for t in others:
                row_part(g, t).wait_send()
            far_sum(g).wait_send()
            for second in (False, True):
                mate_sum(g, second).wait_send()
                mate_sum_wait(g, second)

    return types.SimpleNamespace(
        order=order, everyone=everyone, start=start, start_out=start_out, start_grad=start_grad,
        start_norm=start_norm, stage_far=stage_far, stage_row=stage_row,
        outputs_out=outputs_out, outputs_grad=outputs_grad, grads_home=grads_home,
        norm_rows=norm_rows, norm_cols=norm_cols, norm_last=norm_last, finish=finish,
        spread=spread, drain=drain)


def lane_low(shape):
    return lax.broadcasted_iota(jnp.int32, shape, len(shape) - 1) < HEAD_DIM


def swap(tile):
    return pltpu.roll(tile, HEAD_DIM, 1)


def layer_kernel(row_count, width, groups_out, names, tok, cotan, nrm, seg_ref, freq_ref,
                 w0, w1, w2, w3, out_t, grad_t, nrm_t, r0, r1, r2, r3, *scratch):
    s = types.SimpleNamespace()
    for name, ref in zip(names, scratch):
        if name[-1].isdigit() and name[:-1] in LISTS:
            vars(s).setdefault(name[:-1], []).append(ref)
        else:
            setattr(s, name, ref)
    f32, bf16 = jnp.float32, jnp.bfloat16
    at = places(row_count)
    data, row, col, quarter, far, mate = at
    gat = gatherer(row_count, at, tok, cotan, nrm, (w0, w1, w2, w3), s.whole, s)
    red = reducer(row_count, groups_out, at, s.part, (r0, r1, r2, r3), out_t, grad_t, nrm_t, s)
    wq, wp, wd, wu = s.whole
    gq, gp, gd, gu = s.part
    length = s.xg.shape[1] * 2 // 3
    halflen = length // 2
    attn = wp.shape[1]
    hidden = wu.shape[1]
    last = row_count - 1

    greet([(data, lax.rem(row + k, row_count), col) for k in range(1, row_count)]
          + [(data, row, 1 - col)] + [(t, row, col) for t in red.everyone])

    def mm(a, b):
        return jnp.dot(a, b, preferred_element_type=f32)

    def mm_cols(a, b):
        return lax.dot_general(a, b, (((1,), (1,)), ((), ())), preferred_element_type=f32)

    def mm_rows(a, b):
        return lax.dot_general(a, b, (((0,), (0,)), ((), ())), preferred_element_type=f32)

    gat.begin()
    gat.send_own(0)
    gat.send_own(1)

    seg_row = seg_ref[pl.ds(row, 1), :].astype(f32)
    seg_col = jnp.broadcast_to(seg_row, (8, length)).T[:, 0:1]
    spans, pos = [], []
    for i in range(length // QBLOCK):
        spans.append((i * QBLOCK, max(0, i * QBLOCK - WINDOW), (i + 1) * QBLOCK))
    for n, (start, lo, hi) in enumerate(spans):
        shape = (QBLOCK, hi - lo)
        qi = lax.broadcasted_iota(jnp.int32, shape, 0) + start
        ki = lax.broadcasted_iota(jnp.int32, shape, 1) + lo
        allowed = (seg_col[start:hi] == seg_row[:, lo:hi]) & (ki <= qi)
        seen = jnp.where(allowed, 1.0, 0.0)
        s.mask[n, :, :hi - lo] = seen
        pos.append(jnp.sum(seen, 1, keepdims=True) - 1.0)
    angle = jnp.concatenate(pos, 0) * freq_ref[0:1, :]
    s.cosine[...] = jnp.cos(angle)
    s.sine[...] = jnp.sin(angle)
    lane = lax.rem(lax.broadcasted_iota(jnp.int32, (length, LANES), 1), HEAD_DIM)
    half = ROT_DIM // 2

    def turn(tile, sign):
        sine = s.sine[...]
        up = jnp.where(lane < half, -sine, 0.0)
        down = jnp.where((lane >= half) & (lane < ROT_DIM), sine, 0.0)
        return (tile * s.cosine[...] + sign * (pltpu.roll(tile, LANES - half, 1) * up
                                               + pltpu.roll(tile, half, 1) * down))

    gat.forward(0)
    gat.cot_hop()
    gat.relay(0, 1)
    gat.send_own(2)
    for k in range(2, row_count):
        gat.relay(0, k)
    gat.arrived(0)
    gat.norm_arrived()

    low = lane_low((halflen, LANES))
    lowq = lane_low((length, LANES))
    low8 = lane_low((8, LANES))

    def tiles(ref):
        found = []
        for p in range(row_count // 2):
            left = ref[2 * p, length:, :].astype(f32)
            right = ref[2 * p + 1, length:, :].astype(f32)
            middle = swap(ref[2 * p + 1, :length, :].astype(f32))
            left = jnp.concatenate([left, swap(left)], 0)
            right = jnp.concatenate([swap(right), right], 0)
            found += [ref[2 * p, :length, :].astype(f32), jnp.where(lowq, left, middle),
                      jnp.where(lowq, middle, right)]
        return found

    def norm_tile(n):
        p, place = n // 3, n % 3
        if place == 0:
            return s.ng[2 * p, :, :LANES]
        middle = swap(s.ng[2 * p + 1, :, :LANES])
        if place == 1:
            return jnp.where(low8, s.ng[2 * p, :, LANES:], middle)
        return jnp.where(low8, middle, swap(s.ng[2 * p + 1, :, LANES:]))

    xt = tiles(s.xg)
    mean = sum(jnp.sum(t, 1, keepdims=True) for t in xt) / width
    spread = sum(jnp.sum(t * t, 1, keepdims=True) for t in xt) / width - mean * mean
    rstd = lax.rsqrt(spread + norm_eps)
    for n in range(len(xt)):
        cols = slice(n * LANES, (n + 1) * LANES)
        gain = norm_tile(n)
        value = (xt[n] - mean) * rstd
        s.normed[:, cols] = value
        first = (value * gain[0:1] + gain[1:2]).astype(bf16)
        second = (value * gain[2:3] + gain[3:4]).astype(bf16)
        s.fi[:, cols] = first
        s.si[:, cols] = second
        s.fit[cols, :] = first.T
        s.sit[cols, :] = second.T
    s.rstd[...] = jnp.broadcast_to(rstd, (length, LANES))

    for k in range(1, row_count):
        gat.relay(1, k)
    gat.send_own(3)
    gat.forward(1)
    gat.relay(2, 1)
    gat.landed(0)
    gat.arrived(1)
    ct = tiles(s.cg)
    for n in range(len(ct)):
        cols = slice(n * LANES, (n + 1) * LANES)
        value = ct[n].astype(bf16)
        s.co[:, cols] = value
        s.cot[cols, :] = value.T
    gat.relay(2, 2)
    gat.landed(1)
    s.dcat[...] = mm(s.co[...], wp[...]).astype(bf16)
    lowb = lane_low((QBLOCK, LANES))
    scale = 1.0 / math.sqrt(HEAD_DIM)

    def pair_step(p):
        base = p * 3 * LANES
        out_at = slice(p * LANES, (p + 1) * LANES)
        packed = mm(s.fi[...], wq[:, base:base + 3 * LANES])
        t0, t1, t2 = (packed[:, n * LANES:(n + 1) * LANES] for n in range(3))
        query = turn(jnp.where(lowq, t0, t1), 1.0).astype(bf16)
        keys = turn(swap(jnp.where(lowq, t2, t0)), 1.0).astype(bf16)
        values = jnp.where(lowq, t1, t2).astype(bf16)
        grads = s.dcat[:, out_at]
        s.dk[...] = jnp.zeros_like(s.dk)
        s.dv[...] = jnp.zeros_like(s.dv)
        zero = jnp.zeros((), bf16)
        dqs = []
        for n, (start, lo, hi) in enumerate(spans):
            allowed = s.mask[n, :, :hi - lo] > 0.5
            qb, gb = query[start:hi], grads[start:hi]
            kw, vw = keys[lo:hi], values[lo:hi]
            mixed, dq = [], []
            for head in range(2):
                sel = lowb if head == 0 else jnp.logical_not(lowb)
                qm = jnp.where(sel, qb, zero)
                gm = jnp.where(sel, gb, zero)
                scores = jnp.where(allowed, mm_cols(qm, kw) * scale, mask_fill)
                logsum = jnp.log(jnp.sum(jnp.exp(scores), 1, keepdims=True))
                probs = jnp.exp(scores - logsum)
                weights = probs.astype(bf16)
                got = mm(weights, vw).astype(bf16)
                delta = jnp.sum(gm.astype(f32) * got.astype(f32), 1, keepdims=True)
                prod = mm_cols(gm, vw)
                score_grad = (probs * (prod - delta) * scale).astype(bf16)
                mixed.append(got)
                dq.append(mm(score_grad, kw))
                s.dk[lo:hi, :] += mm_rows(score_grad, qm)
                s.dv[lo:hi, :] += mm_rows(weights, gm)
            s.att[start:hi, out_at] = jnp.where(lowb, mixed[0], mixed[1])
            dqs.append(jnp.where(lowb, dq[0], dq[1]))
        dquery = turn(jnp.concatenate(dqs, 0), -1.0)
        dkeys = swap(turn(s.dk[...], -1.0))
        dvals = s.dv[...]
        s.pg[:, base:base + LANES] = jnp.where(lowq, dquery, dkeys).astype(bf16)
        s.pg[:, base + LANES:base + 2 * LANES] = jnp.where(lowq, dvals, dquery).astype(bf16)
        s.pg[:, base + 2 * LANES:base + 3 * LANES] = jnp.where(lowq, dkeys, dvals).astype(bf16)

    todo = [(2, k) for k in range(3, row_count)] + [(3, k) for k in range(1, row_count)]
    for p in range(attn // LANES):
        pair_step(p)
        if todo:
            gat.relay(*todo.pop(0))
    step = 2 * LANES

    def weight_grads(ref, left, right, size):
        count = size // step

        def one(n, carry):
            cols = pl.ds(pl.multiple_of(n * step, step), step)
            ref[:, cols] = mm(left[...], right[:, cols]).astype(bf16)
            return carry

        lax.fori_loop(0, count, one, 0)
        if size % step:
            cols = slice(count * step, size)
            ref[:, cols] = mm(left[...], right[:, cols]).astype(bf16)

    weight_grads(gq, s.fit, s.pg, s.pg.shape[1])
    red.start(0)
    while todo:
        gat.relay(*todo.pop(0))
    weight_grads(gp, s.cot, s.att, attn)
    red.start(1)
    for t in red.order:
        red.stage_far(0, t)
    gat.settle()
    gat.landed(2)
    gat.landed(3)
    for t in red.order:
        red.stage_far(1, t)

    def hidden_step(n, carry):
        cols = pl.ds(pl.multiple_of(n * step, step), step)
        value = mm(s.si[...], wu[:, cols])
        erf = 0.5 * (1.0 + lax.erf(value * inv_sqrt_two))
        s.act[:, cols] = (value * erf).astype(bf16)
        slope = erf + value * inv_sqrt_two_pi * jnp.exp(-0.5 * value * value)
        s.hg[:, cols] = (mm(s.co[...], wd[:, cols]) * slope).astype(bf16)
        return carry

    lax.fori_loop(0, hidden // step, hidden_step, 0)
    weight_grads(gd, s.cot, s.act, hidden)
    red.start(2)
    weight_grads(gu, s.sit, s.hg, hidden)
    red.start(3)
    for g in (2, 3):
        for t in red.order:
            red.stage_far(g, t)

    def put_tiles(ref, chunks):
        for p in range(row_count // 2):
            t0, t1, t2 = chunks[3 * p:3 * p + 3]
            ref[2 * p, :length, :] = t0.astype(bf16)
            ref[2 * p + 1, :length, :] = swap(jnp.where(lowq, t2, t1)).astype(bf16)
            ref[2 * p, length:, :] = jnp.where(
                low, t1[:halflen], swap(t1[halflen:])).astype(bf16)
            ref[2 * p + 1, length:, :] = jnp.where(
                low, swap(t2[:halflen]), t2[halflen:]).astype(bf16)

    def split(value):
        return [value[:, n * LANES:(n + 1) * LANES] for n in range(value.shape[1] // LANES)]

    out_tiles = []
    for n in range(width // step):
        cols = slice(n * step, (n + 1) * step)
        out_tiles += split(mm_cols(s.att[...], wp[cols, :]) + mm_cols(s.act[...], wd[cols, :]))
    put_tiles(s.outp, out_tiles)
    red.start_out()
    for t in red.order:
        red.stage_row(0, t)
    back1, back2 = 0.0, 0.0
    sums = []
    for n in range(width // step):
        cols = slice(n * step, (n + 1) * step)
        first = mm_cols(s.pg[...], wq[cols, :])
        second = mm_cols(s.hg[...], wu[cols, :])
        value = s.normed[:, cols]
        gains = jnp.concatenate([norm_tile(2 * n), norm_tile(2 * n + 1)], 1)
        four = jnp.concatenate(
            [jnp.sum(first * value, 0, keepdims=True), jnp.sum(first, 0, keepdims=True),
             jnp.sum(second * value, 0, keepdims=True), jnp.sum(second, 0, keepdims=True),
             jnp.zeros((4, step), f32)], 0)
        sums += split(four)
        both = gains[0:1] * first + gains[2:3] * second
        s.comb[:, cols] = both
        back1 = back1 + jnp.sum(both, 1, keepdims=True)
        back2 = back2 + jnp.sum(both * value, 1, keepdims=True)
    for p in range(row_count // 2):
        t0, t1, t2 = sums[3 * p:3 * p + 3]
        s.nrmp[2 * p, :, :LANES] = t0
        s.nrmp[2 * p, :, LANES:] = t1
        s.nrmp[2 * p + 1, :, :LANES] = swap(jnp.where(low8, t2, t1))
        s.nrmp[2 * p + 1, :, LANES:] = swap(t2)
    red.start_norm()
    grad_tiles = []
    factor = s.rstd[...]
    for n in range(width // LANES):
        cols = slice(n * LANES, (n + 1) * LANES)
        grad_tiles.append(factor * (
            s.comb[:, cols] - back1 / width - s.normed[:, cols] * (back2 / width)))
    put_tiles(s.gradp, grad_tiles)
    red.start_grad()

    red.outputs_out()
    for t in red.order:
        red.stage_row(1, t)
    red.finish(0)
    red.outputs_grad()
    for t in red.order:
        red.stage_row(2, t)
    red.finish(1)
    red.norm_rows()
    red.spread(0)
    for n, t in enumerate(red.order):
        red.stage_row(3, t)
        if n == 1:
            red.norm_cols()
        if n == last:
            red.finish(2)
    red.grads_home()
    red.spread(1)
    red.finish(3)
    red.norm_last()
    red.spread(2)
    red.spread(3)
    gat.drain()
    red.drain()


LISTS = ("whole", "part", "crecv", "fsend", "frecv", "zsend", "zrecv", "extra")


def layer_all(row_count, data_count, width, tok, cot, nrm, segs, freq, own):
    n = row_count
    bf16, f32 = jnp.bfloat16, jnp.float32
    dma = pltpu.SemaphoreType.DMA
    vmem = pl.BlockSpec(memory_space=pltpu.VMEM)
    anywhere = pl.BlockSpec(memory_space=pl.ANY)
    shares, rows, _ = tok.shape
    length = segs.shape[1]
    groups = len(own)
    groups_out = data_count // QUARTERS
    sizes = [w.shape[1] for w in own]
    local = own[0].shape[0]
    depth = local // QUARTERS
    block = (rows, LANES)
    small = nrm.shape
    attn, hidden = sizes[1], sizes[3]
    spec = {}

    def buffers(dtype, **shapes):
        for name, shape in shapes.items():
            spec[name] = pltpu.VMEM(shape, dtype)

    def each(name, lead):
        for g, size in enumerate(sizes):
            spec[f"{name}{g}"] = pltpu.VMEM(lead + (size,), bf16)

    def sems(**shapes):
        for name, shape in shapes.items():
            spec[name] = dma(shape)

    each("whole", (width,))
    each("part", (width,))
    each("crecv", (2, n, depth))
    for name in ("fsend", "frecv", "zsend", "zrecv"):
        each(name, (n, depth))
    each("extra", (groups_out, depth))
    buffers(bf16, xg=(n,) + block, cg=(n,) + block, hop=(shares,) + block,
            fi=(length, width), si=(length, width), co=(length, width),
            fit=(width, length), sit=(width, length), cot=(width, length),
            dcat=(length, attn), att=(length, attn), act=(length, hidden), hg=(length, hidden),
            pg=(length, sizes[0]), outp=(n,) + block, gradp=(n,) + block,
            oy=(n,) + block, od=(n,) + block, gy=(n,) + block, gd=(n,) + block,
            gh=(shares,) + block)
    buffers(f32, ng=(n,) + small, nrmp=(n,) + small, nz=(n,) + small, nc=small, nrm1=small,
            nrm2=small, nd=(data_count,) + small, mask=(length // QBLOCK, QBLOCK, WINDOW + QBLOCK),
            cosine=(length, LANES), sine=(length, LANES), rstd=(length, LANES),
            dk=(length, LANES), dv=(length, LANES), normed=(length, width),
            comb=(length, width))
    sems(nrm_s=(n,), nrm_r=(n,), x_s=(shares,), x_r=(n,), xy_s=(n,), xy_r=(n,),
         h_s=(shares,), h_r=(shares,), c_s=(shares,), c_r=(n,), cy_s=(n,), cy_r=(n,),
         loc=(5,), own_l=(groups,), z_s=(2, groups, n), z_r=(groups, n),
         f_s=(groups, n), f_r=(groups, n), m_s=(2, groups, n), m_r=(2, groups, n),
         oy_s=(n,), oy_r=(n,), oz_s=(n,), oz_r=(shares,), gy_s=(n,), gy_r=(n,),
         gz_s=(n,), gz_r=(shares,), gh_s=(shares,), gh_r=(shares,), nz_s=(n,), nz_r=(n,),
         nc_s=(1,), nc_r=(1,), nd_s=(data_count,), nd_r=(data_count,),
         pc_s=(2, groups, n), pc_r=(2, groups, n), pf_s=(groups, n), pf_r=(groups, n),
         pz_s=(groups, n), pz_r=(groups, n), e_s=(groups, groups_out), e_r=(groups, groups_out),
         a_s=(groups,), a_r=(groups,), b_s=(2, groups), b_r=(2, groups))
    return pl.pallas_call(
        functools.partial(layer_kernel, n, width, groups_out, tuple(spec)),
        out_shape=[
            jax.ShapeDtypeStruct((shares,) + block, bf16),
            jax.ShapeDtypeStruct((shares,) + block, bf16),
            jax.ShapeDtypeStruct(small, f32),
        ] + [jax.ShapeDtypeStruct((local, size), bf16) for size in sizes],
        in_specs=[anywhere] * 3 + [vmem] * 2 + [anywhere] * groups,
        out_specs=[vmem] * (3 + groups),
        scratch_shapes=list(spec.values()),
        compiler_params=pltpu.CompilerParams(
            collective_id=0, has_side_effects=True, vmem_limit_bytes=63 << 20
        ),
        name="layer",
    )(tok, cot, nrm, segs, freq, *own)


def pack_tokens(rows, length):
    blocks = rows.reshape(-1, length, rows.shape[1])
    ends = blocks[:, :, LANES:]
    joined = jnp.concatenate([ends[:, :length // 2], ends[:, length // 2:]], 2)
    return jnp.concatenate([blocks[:, :, :LANES], joined], 1)


def unpack_tokens(blocks, length):
    joined = blocks[:, length:]
    small = joined.shape[2] // 2
    ends = jnp.concatenate([joined[:, :, :small], joined[:, :, small:]], 1)
    return jnp.concatenate([blocks[:, :length], ends], 2).reshape(-1, LANES + small)


def on_device(
    tokens_in,
    out_cot,
    segments,
    norm_params,
    qkv_weight,
    proj_weight,
    up_weight,
    down_weight,
    norm_first,
    norm_second,
    qkv_first,
    qkv_second,
    proj_first,
    proj_second,
    up_first,
    up_second,
    down_first,
    down_second,
):
    row_count = lax.axis_size("row")
    data_count = lax.axis_size("dp")
    col_count = lax.axis_size("col")
    local_count, local_width = tokens_in.shape
    width = local_width * row_count
    length = segments.shape[1]
    shares = local_count // length
    bf16 = jnp.bfloat16

    own = (
        qkv_weight.astype(bf16),
        proj_weight.T.astype(bf16),
        down_weight.T.astype(bf16),
        up_weight.astype(bf16),
    )
    nrm = jnp.pad(norm_params, ((0, 4), (0, 2 * LANES - local_width)))
    half = ROT_DIM // 2
    freq = rotary_base ** (-2.0 * jnp.arange(half, dtype=jnp.float32) / ROT_DIM)
    freq = jnp.concatenate([freq, freq, jnp.zeros(HEAD_DIM - ROT_DIM, jnp.float32)])
    freq = jnp.broadcast_to(jnp.tile(freq, 2)[None], (8, LANES))
    out_sum, grad_sum, norm_sum, qkv_sum, proj_sum, down_sum, up_sum = layer_all(
        row_count, data_count, width, pack_tokens(tokens_in, length),
        pack_tokens(out_cot, length), nrm, segments, freq, own)

    output = (tokens_in.astype(jnp.float32)
              + unpack_tokens(out_sum, length).astype(jnp.float32)).astype(bf16)
    input_grad = (out_cot.astype(jnp.float32)
                  + unpack_tokens(grad_sum, length).astype(jnp.float32)).astype(bf16)
    norm_grad = norm_sum[:4, :local_width]
    qkv_grad = qkv_sum.astype(jnp.float32)
    up_grad = up_sum.astype(jnp.float32)
    proj_grad = proj_sum.astype(jnp.float32).T
    down_grad = down_sum.astype(jnp.float32).T
    norm_new, norm_first_new, norm_second_new = adam_update(
        norm_params, norm_first, norm_second, norm_grad, 0.0
    )
    qkv_new, qkv_first_new, qkv_second_new = adam_update(
        qkv_weight, qkv_first, qkv_second, qkv_grad, decay_rate
    )
    proj_new, proj_first_new, proj_second_new = adam_update(
        proj_weight, proj_first, proj_second, proj_grad, decay_rate
    )
    up_new, up_first_new, up_second_new = adam_update(
        up_weight, up_first, up_second, up_grad, decay_rate
    )
    down_new, down_first_new, down_second_new = adam_update(
        down_weight, down_first, down_second, down_grad, decay_rate
    )
    return (
        output,
        input_grad,
        norm_grad,
        qkv_grad,
        proj_grad,
        up_grad,
        down_grad,
        norm_new,
        qkv_new,
        proj_new,
        up_new,
        down_new,
        norm_first_new,
        norm_second_new,
        qkv_first_new,
        qkv_second_new,
        proj_first_new,
        proj_second_new,
        up_first_new,
        up_second_new,
        down_first_new,
        down_second_new,
    )


def solution(mesh):
    placed = (
        P(("dp", "col"), "row"),
        P(("dp", "col"), "row"),
        P("dp", None),
        P(None, "row"),
        P("row", "col"),
        P("col", "row"),
        P("row", "col"),
        P("col", "row"),
        P(None, "row"),
        P(None, "row"),
        P("row", "col"),
        P("row", "col"),
        P("col", "row"),
        P("col", "row"),
        P("row", "col"),
        P("row", "col"),
        P("col", "row"),
        P("col", "row"),
    )
    return jax.shard_map(
        on_device,
        mesh=mesh,
        in_specs=placed,
        out_specs=(
            P(("dp", "col"), "row"),
            P(("dp", "col"), "row"),
            P(None, "row"),
            P("row", "col"),
            P("col", "row"),
            P("row", "col"),
            P("col", "row"),
            P(None, "row"),
            P("row", "col"),
            P("col", "row"),
            P("row", "col"),
            P("col", "row"),
            P(None, "row"),
            P(None, "row"),
            P("row", "col"),
            P("row", "col"),
            P("col", "row"),
            P("col", "row"),
            P("row", "col"),
            P("row", "col"),
            P("col", "row"),
            P("col", "row"),
        ),
        check_vma=False,
    )
```

time: 317 us -> 198 us (0.62)
  Pallas kernels: 0 us -> 171 us
  blocking collectives: 141 us -> 0 us
  matrix products: 47.2 us -> 0 us
  local copies, waits for them, and re-layouts: 42.1 us -> 7.94 us
  waiting for transfers between devices: 21.7 us -> 0 us
  starting transfers between devices: 21 us -> 0 us
  between operations: 15.2 us -> 0.95 us
  other arithmetic: 25.5 us -> 17.8 us
    pallas_call x0 -> x1, Pallas kernels: none -> 171 us  [layer_all(): pl.pallas_call(functools.partial(layer_kernel, n, width, groups_out, tupl...]
    all_gather x6 -> x0, blocking collectives: 83.4 us -> none  [the longest x1 40.2 us: on_device(): norm_full = lax.all_gather(norm_params, 'row', axis=1, tiled=True)]
    psum x1 -> x0, blocking collectives: 57.2 us -> none  [on_device(): lax.psum(norm_part, ('dp', 'row', 'col'))]
    dot_general x14 -> x0, matrix products: 39.8 us -> none  [the longest x3 12.5 us: dot32(): return jnp.dot(left, right, preferred_element_type=jnp.float32)]
    all_to_all x4 -> x0, starting transfers between devices: 16.6 us -> none  [the longest x2 9.31 us: to_tokens(): blocks = lax.all_to_all(blocks, 'row', 0, 0, tiled=True)]
    unnamed x96 -> x52, local copies, waits for them, and re-layouts: 21 us -> 4.56 us
    all_to_all x4 -> x0, waiting for transfers between devices: 15.9 us -> none  [the longest x2 11.4 us: to_features(): blocks = lax.all_to_all(jnp.moveaxis(blocks, 1, 0), 'row', 0, 0, tiled=True)]
    convert_element_type x6 -> x2, local copies, waits for them, and re-layouts: 9.14 us -> 0.63 us  [the longest x1 0.31 us: on_device(): unpack_tokens(grad_sum, length).astype(jnp.float32)]
  transfers between devices with their start and end apart: 8 -> 0, of which waited for: 3 -> 0; matrix products, arithmetic and copies ran while one was open for 12% -> 0% of each run, Pallas kernels for 0% -> 0%
where the time goes in v2:
time: 198 us; the launch traced here: 197 us
  Pallas kernels  171 us (86%)
  other arithmetic  17.8 us (9%)
  local copies, waits for them, and re-layouts  7.94 us (4%)
    pallas_call x1, Pallas kernels, layer_all(): pl.pallas_call(functools.partial(layer_kernel, n, width, groups_out, tupl...  171 us
    sub x5, other arithmetic, adam_update(): weight - learn_rate * (first_hat / (jnp.sqrt(second_hat) + adam_eps) + de...  10.7 us
    unnamed x52, local copies, waits for them, and re-layouts  4.56 us

profile of v2, /device:TPU:0, one launch (start us, length us, event | category | flops | bytes accessed | tf_op | source)
XLA Modules:
  0.0 197.2 jit_solution(17874986061586369050)
XLA Ops:
  0.7 1.2 copy.41
  2.0 0.9 maximum_maximum_fusion.3.cotan
  3.2 0.9 maximum_maximum_fusion.2.tok
  4.0 0.5 copy-done
  4.5 0.9 convert_bitcast_fusion.1.w2
  5.4 0.9 convert_element_type.56.w3
  6.2 0.5 copy-done.4
  6.7 0.8 convert_element_type.51.w0
  7.6 0.7 convert_bitcast_fusion.3.w1
  8.2 0.6 pad.4.nrm
  9.0 0.6 broadcast_in_dim.12.freq_ref
  9.6 170.5 %layer.1 = (bf16[2,768,128]{2,1,0:T(8,128)(2,1)}, bf16[2,768,128]{2,1,0:T(8,128)(2,1)}, f32[8,256]{1,0:T(8,128)}, bf16[192,1152]{1,0:T(8,128)(2,1)}, bf16[192,38...) custom-call(bf16[2,768,128]{2,1,0:T(8,128)(2,1)} %maximum_maximum_fusion.2.tok, ...), custom_call_target="tpu_custom_call" | custom-call | tf_op jit(solution)/shard_map/layer/pallas_call | solution.py:967
  180.2 1.3 fusion.12
  181.7 0.3 copy.43
  182.1 0.7 copy-done.5
  182.7 0.8 add_convert_fusion
  184.3 0.7 copy-done.7
  185.0 0.8 add_convert_fusion.1
  185.8 0.6 copy-done.1
  186.4 4.5 %multiply_subtract_fusion = (f32[1536,192]{0,1:T(8,128)}, f32[1536,192]{0,1:T(8,128)}, f32[1536,192]{0,1:T(8,128)}, f32[1536,192]{0,1:T(8,128)}) fusion(f32[1536,192]{0,1:T(8,128)S(1)} %copy-done.1, f32[1536,192]{0,1:T(8,128)} %param.34, f32[1536,192]{0,1:T(8,128)} %param.35, bf16[192,1536]{1,0:T(8,128)(2,1)} %get-tuple-element.35), kind=kLoop, calls=%fused_computation.6 | loop fusion | flops 4718592 | bytes 8847360 | tf_op jit(solution)/shard_map/sub | solution.py:36
  190.9 2.6 %multiply_subtract_fusion.1 = (f32[192,1536]{1,0:T(8,128)}, f32[192,1536]{1,0:T(8,128)}, f32[192,1536]{1,0:T(8,128)}, f32[192,1536]{1,0:T(8,128)}) fusion(f32[192,1536]{1,0:T(8,128)S(1)} %copy-done.3, f32[192,1536]{1,0:T(8,128)S(1)} %copy-done.8, f32[192,1536]{1,0:T(8,128)S(1)} %copy-done.9, bf16[192,1536]{1,0:T(8,128)(2,1)S(1)} %copy-done.16), kind=kLoop, calls=%fused_computation.8 | loop fusion | flops 4718592 | bytes 8847360 | tf_op jit(solution)/shard_map/sub | solution.py:36
  193.5 2.0 multiply_subtract_fusion.2
  195.5 1.1 multiply_subtract_fusion.3
  196.6 0.6 multiply_subtract_fusion.4
  (62 shorter events, 1.6 us)
Async XLA Ops:
  1.9 1.0 copy-start.6
  3.1 1.4 copy-start
  3.2 2.2 %copy-start.2 = (f32[192,1536]{1,0:T(8,128)S(1)}, f32[192,1536]{1,0:T(8,128)}, u32[]{:S(2)}) copy-start(f32[192,1536]{1,0:T(8,128)} %param.24) | copy-start | bytes 3538948
  5.4 1.4 copy-start.4
  5.4 2.2 %copy-start.10 = (f32[384,192]{0,1:T(8,128)S(1)}, f32[384,192]{0,1:T(8,128)}, u32[]{:S(2)}) copy-start(f32[384,192]{0,1:T(8,128)} %param.23) | copy-start | bytes 884740
  6.7 1.5 copy-start.21
  180.2 1.3 copy-start.15
  181.7 1.0 copy-start.5
  184.0 1.0 copy-start.7
  185.0 1.4 copy-start.1
  186.4 4.5 %copy-start.3 = (f32[192,1536]{1,0:T(8,128)S(1)}, f32[192,1536]{1,0:T(8,128)}, u32[]{:S(2)}) copy-start(f32[192,1536]{1,0:T(8,128)} %param.24) | copy-start | bytes 3538948
  186.4 4.5 %copy-start.8 = (f32[192,1536]{1,0:T(8,128)S(1)}, f32[192,1536]{1,0:T(8,128)}, u32[]{:S(2)}) copy-start(f32[192,1536]{1,0:T(8,128)} %param.32) | copy-start | bytes 3538948
  186.4 4.5 %copy-start.9 = (f32[192,1536]{1,0:T(8,128)S(1)}, f32[192,1536]{1,0:T(8,128)}, u32[]{:S(2)}) copy-start(f32[192,1536]{1,0:T(8,128)} %param.33) | copy-start | bytes 3538948
  186.4 4.5 %copy-start.16 = (bf16[192,1536]{1,0:T(8,128)(2,1)S(1)}, bf16[192,1536]{1,0:T(8,128)(2,1)}, u32[]{:S(2)}) copy-start(bf16[192,1536]{1,0:T(8,128)(2,1)} %get-tuple-element.34) | copy-start | bytes 1769476
  190.9 2.6 %copy-start.12 = (f32[192,1152]{1,0:T(8,128)S(1)}, f32[192,1152]{1,0:T(8,128)}, u32[]{:S(2)}) copy-start(f32[192,1152]{1,0:T(8,128)} %param.28) | copy-start | bytes 2654212
  190.9 2.6 %copy-start.13 = (f32[192,1152]{1,0:T(8,128)S(1)}, f32[192,1152]{1,0:T(8,128)}, u32[]{:S(2)}) copy-start(f32[192,1152]{1,0:T(8,128)} %param.29) | copy-start | bytes 2654212
  190.9 2.6 %copy-start.17 = (bf16[192,1152]{1,0:T(8,128)(2,1)S(1)}, bf16[192,1152]{1,0:T(8,128)(2,1)}, u32[]{:S(2)}) copy-start(bf16[192,1152]{1,0:T(8,128)(2,1)} %get-tuple-element.32) | copy-start | bytes 1327108
  193.5 2.0 %copy-start.11 = (f32[384,192]{0,1:T(8,128)S(1)}, f32[384,192]{0,1:T(8,128)}, u32[]{:S(2)}) copy-start(f32[384,192]{0,1:T(8,128)} %param.23) | copy-start | bytes 884740
  193.5 2.0 %copy-start.18 = (f32[384,192]{0,1:T(8,128)S(1)}, f32[384,192]{0,1:T(8,128)}, u32[]{:S(2)}) copy-start(f32[384,192]{0,1:T(8,128)} %param.30) | copy-start | bytes 884740
  193.5 2.0 %copy-start.19 = (f32[384,192]{0,1:T(8,128)S(1)}, f32[384,192]{0,1:T(8,128)}, u32[]{:S(2)}) copy-start(f32[384,192]{0,1:T(8,128)} %param.31) | copy-start | bytes 884740
  193.5 2.0 %copy-start.20 = (bf16[192,384]{1,0:T(8,128)(2,1)S(1)}, bf16[192,384]{1,0:T(8,128)(2,1)}, u32[]{:S(2)}) copy-start(bf16[192,384]{1,0:T(8,128)(2,1)} %get-tuple-element.33) | copy-start | bytes 442372
  195.5 1.1 copy-start.22
  195.5 1.1 copy-start.23
  195.5 1.1 copy-start.24
  (1 other events, 1.0 us)

commit v3 on v2

--- a/solution.py
+++ b/solution.py
@@ -658,9 +658,9 @@
         return (tile * s.cosine[...] + sign * (pltpu.roll(tile, LANES - half, 1) * up
                                                + pltpu.roll(tile, half, 1) * down))
 
-    gat.forward(0)
     gat.cot_hop()
     gat.relay(0, 1)
+    gat.forward(0)
     gat.send_own(2)
     for k in range(2, row_count):
         gat.relay(0, k)
@@ -799,11 +799,11 @@
     red.start(1)
     for t in red.order:
         red.stage_far(0, t)
+    for t in red.order:
+        red.stage_far(1, t)
     gat.settle()
     gat.landed(2)
     gat.landed(3)
-    for t in red.order:
-        red.stage_far(1, t)
 
     def hidden_step(n, carry):
         cols = pl.ds(pl.multiple_of(n * step, step), step)
@@ -817,11 +817,16 @@
     lax.fori_loop(0, hidden // step, hidden_step, 0)
     weight_grads(gd, s.cot, s.act, hidden)
     red.start(2)
+    for t in red.order:
+        red.stage_row(0, t)
+    for t in red.order:
+        red.stage_far(2, t)
     weight_grads(gu, s.sit, s.hg, hidden)
     red.start(3)
-    for g in (2, 3):
-        for t in red.order:
-            red.stage_far(g, t)
+    for t in red.order:
+        red.stage_row(1, t)
+    for t in red.order:
+        red.stage_far(3, t)
 
     def put_tiles(ref, chunks):
         for p in range(row_count // 2):
@@ -842,8 +847,6 @@
         out_tiles += split(mm_cols(s.att[...], wp[cols, :]) + mm_cols(s.act[...], wd[cols, :]))
     put_tiles(s.outp, out_tiles)
     red.start_out()
-    for t in red.order:
-        red.stage_row(0, t)
     back1, back2 = 0.0, 0.0
     sums = []
     for n in range(width // step):
@@ -878,12 +881,10 @@
     red.start_grad()
 
     red.outputs_out()
-    for t in red.order:
-        red.stage_row(1, t)
     red.finish(0)
-    red.outputs_grad()
     for t in red.order:
         red.stage_row(2, t)
+    red.outputs_grad()
     red.finish(1)
     red.norm_rows()
     red.spread(0)

time: 198 us -> 194 us (0.980); the launches traced: 197 us -> 191 us
  Pallas kernels: 171 us -> 164 us
    pallas_call x1, Pallas kernels: 171 us -> 164 us  [layer_all(): pl.pallas_call(functools.partial(layer_kernel, n, width, groups_out, tupl...]
where the time goes in v3:
time: 194 us; the launch traced here: 191 us
  Pallas kernels  164 us (85%)
  other arithmetic  17.8 us (9%)
  local copies, waits for them, and re-layouts  7.94 us (4%)
    pallas_call x1, Pallas kernels, layer_all(): pl.pallas_call(functools.partial(layer_kernel, n, width, groups_out, tupl...  164 us
    sub x5, other arithmetic, adam_update(): weight - learn_rate * (first_hat / (jnp.sqrt(second_hat) + adam_eps) + de...  10.7 us
    unnamed x52, local copies, waits for them, and re-layouts  4.56 us

profile of v3, /device:TPU:0, one launch (start us, length us, event | category | flops | bytes accessed | tf_op | source)
XLA Modules:
  0.0 191.1 jit_solution(7291740910481426147)
XLA Ops:
  0.7 1.2 copy.41
  2.0 0.9 maximum_maximum_fusion.3.cotan
  3.2 0.9 maximum_maximum_fusion.2.tok
  4.0 0.5 copy-done
  4.5 0.9 convert_bitcast_fusion.1.w2
  5.4 0.9 convert_element_type.56.w3
  6.2 0.5 copy-done.4
  6.7 0.8 convert_element_type.51.w0
  7.6 0.7 convert_bitcast_fusion.3.w1
  8.2 0.6 pad.4.nrm
  9.0 0.6 broadcast_in_dim.12.freq_ref
  9.6 164.4 %layer.1 = (bf16[2,768,128]{2,1,0:T(8,128)(2,1)}, bf16[2,768,128]{2,1,0:T(8,128)(2,1)}, f32[8,256]{1,0:T(8,128)}, bf16[192,1152]{1,0:T(8,128)(2,1)}, bf16[192,38...) custom-call(bf16[2,768,128]{2,1,0:T(8,128)(2,1)} %maximum_maximum_fusion.2.tok, ...), custom_call_target="tpu_custom_call" | custom-call | tf_op jit(solution)/shard_map/layer/pallas_call | solution.py:968
  174.1 1.3 fusion.12
  175.6 0.3 copy.43
  175.9 0.7 copy-done.5
  176.6 0.8 add_convert_fusion
  178.2 0.7 copy-done.7
  178.8 0.8 add_convert_fusion.1
  179.7 0.6 copy-done.1
  180.3 4.5 %multiply_subtract_fusion = (f32[1536,192]{0,1:T(8,128)}, f32[1536,192]{0,1:T(8,128)}, f32[1536,192]{0,1:T(8,128)}, f32[1536,192]{0,1:T(8,128)}) fusion(f32[1536,192]{0,1:T(8,128)S(1)} %copy-done.1, f32[1536,192]{0,1:T(8,128)} %param.34, f32[1536,192]{0,1:T(8,128)} %param.35, bf16[192,1536]{1,0:T(8,128)(2,1)} %get-tuple-element.35), kind=kLoop, calls=%fused_computation.6 | loop fusion | flops 4718592 | bytes 8847360 | tf_op jit(solution)/shard_map/sub | solution.py:36
  184.8 2.6 %multiply_subtract_fusion.1 = (f32[192,1536]{1,0:T(8,128)}, f32[192,1536]{1,0:T(8,128)}, f32[192,1536]{1,0:T(8,128)}, f32[192,1536]{1,0:T(8,128)}) fusion(f32[192,1536]{1,0:T(8,128)S(1)} %copy-done.3, f32[192,1536]{1,0:T(8,128)S(1)} %copy-done.8, f32[192,1536]{1,0:T(8,128)S(1)} %copy-done.9, bf16[192,1536]{1,0:T(8,128)(2,1)S(1)} %copy-done.16), kind=kLoop, calls=%fused_computation.8 | loop fusion | flops 4718592 | bytes 8847360 | tf_op jit(solution)/shard_map/sub | solution.py:36
  187.4 2.0 %multiply_subtract_fusion.2 = (f32[192,1152]{1,0:T(8,128)}, f32[192,1152]{1,0:T(8,128)}, f32[192,1152]{1,0:T(8,128)}, f32[192,1152]{1,0:T(8,128)}) fusion(f32[192,1152]{1,0:T(8,128)S(1)} %copy-done.4, f32[192,1152]{1,0:T(8,128)S(1)} %copy-done.12, f32[192,1152]{1,0:T(8,128)S(1)} %copy-done.13, bf16[192,1152]{1,0:T(8,128)(2,1)S(1)} %copy-done.17), kind=kLoop, calls=%fused_computation.11 | loop fusion | flops 3538944 | bytes 6635520 | tf_op jit(solution)/shard_map/sub | solution.py:36
  189.4 1.1 multiply_subtract_fusion.3
  190.5 0.6 multiply_subtract_fusion.4
  (62 shorter events, 1.6 us)
Async XLA Ops:
  1.9 1.0 copy-start.6
  3.1 1.4 copy-start
  3.2 2.2 %copy-start.2 = (f32[192,1536]{1,0:T(8,128)S(1)}, f32[192,1536]{1,0:T(8,128)}, u32[]{:S(2)}) copy-start(f32[192,1536]{1,0:T(8,128)} %param.24) | copy-start | bytes 3538948
  5.4 1.4 copy-start.4
  5.4 2.2 %copy-start.10 = (f32[384,192]{0,1:T(8,128)S(1)}, f32[384,192]{0,1:T(8,128)}, u32[]{:S(2)}) copy-start(f32[384,192]{0,1:T(8,128)} %param.23) | copy-start | bytes 884740
  6.7 1.5 copy-start.21
  174.0 1.3 copy-start.15
  175.6 1.0 copy-start.5
  177.8 1.0 copy-start.7
  178.8 1.4 copy-start.1
  180.3 4.5 %copy-start.3 = (f32[192,1536]{1,0:T(8,128)S(1)}, f32[192,1536]{1,0:T(8,128)}, u32[]{:S(2)}) copy-start(f32[192,1536]{1,0:T(8,128)} %param.24) | copy-start | bytes 3538948
  180.3 4.5 %copy-start.8 = (f32[192,1536]{1,0:T(8,128)S(1)}, f32[192,1536]{1,0:T(8,128)}, u32[]{:S(2)}) copy-start(f32[192,1536]{1,0:T(8,128)} %param.32) | copy-start | bytes 3538948
  180.3 4.5 %copy-start.9 = (f32[192,1536]{1,0:T(8,128)S(1)}, f32[192,1536]{1,0:T(8,128)}, u32[]{:S(2)}) copy-start(f32[192,1536]{1,0:T(8,128)} %param.33) | copy-start | bytes 3538948
  180.3 4.5 %copy-start.16 = (bf16[192,1536]{1,0:T(8,128)(2,1)S(1)}, bf16[192,1536]{1,0:T(8,128)(2,1)}, u32[]{:S(2)}) copy-start(bf16[192,1536]{1,0:T(8,128)(2,1)} %get-tuple-element.34) | copy-start | bytes 1769476
  184.8 2.6 %copy-start.12 = (f32[192,1152]{1,0:T(8,128)S(1)}, f32[192,1152]{1,0:T(8,128)}, u32[]{:S(2)}) copy-start(f32[192,1152]{1,0:T(8,128)} %param.28) | copy-start | bytes 2654212
  184.8 2.6 %copy-start.13 = (f32[192,1152]{1,0:T(8,128)S(1)}, f32[192,1152]{1,0:T(8,128)}, u32[]{:S(2)}) copy-start(f32[192,1152]{1,0:T(8,128)} %param.29) | copy-start | bytes 2654212
  184.8 2.6 %copy-start.17 = (bf16[192,1152]{1,0:T(8,128)(2,1)S(1)}, bf16[192,1152]{1,0:T(8,128)(2,1)}, u32[]{:S(2)}) copy-start(bf16[192,1152]{1,0:T(8,128)(2,1)} %get-tuple-element.32) | copy-start | bytes 1327108
  187.4 2.0 %copy-start.11 = (f32[384,192]{0,1:T(8,128)S(1)}, f32[384,192]{0,1:T(8,128)}, u32[]{:S(2)}) copy-start(f32[384,192]{0,1:T(8,128)} %param.23) | copy-start | bytes 884740
  187.4 2.0 %copy-start.18 = (f32[384,192]{0,1:T(8,128)S(1)}, f32[384,192]{0,1:T(8,128)}, u32[]{:S(2)}) copy-start(f32[384,192]{0,1:T(8,128)} %param.30) | copy-start | bytes 884740
  187.4 2.0 %copy-start.19 = (f32[384,192]{0,1:T(8,128)S(1)}, f32[384,192]{0,1:T(8,128)}, u32[]{:S(2)}) copy-start(f32[384,192]{0,1:T(8,128)} %param.31) | copy-start | bytes 884740
  187.4 2.0 %copy-start.20 = (bf16[192,384]{1,0:T(8,128)(2,1)S(1)}, bf16[192,384]{1,0:T(8,128)(2,1)}, u32[]{:S(2)}) copy-start(bf16[192,384]{1,0:T(8,128)(2,1)} %get-tuple-element.33) | copy-start | bytes 442372
  189.4 1.1 copy-start.22
  189.4 1.1 copy-start.23
  189.4 1.1 copy-start.24
  (1 other events, 1.0 us)
